TPU v7x, 32 devices: a whole 2x2x4 slice. The times are simulated.
32 devices in a mesh: dp: 8 (over z, x), tensor: 4 (over y, core).
Axes of the slice: x: 2, y: 2, z: 4, core: 2. Of those that a mesh axis runs over, the one named last changes fastest.
Arguments:
- block_input: bfloat16 [4096, 2048], P('dp', 'tensor'), may hold values from -6 to 6
- grad_output: bfloat16 [4096, 2048], P('dp', 'tensor'), may hold values from -6 to 6
- norm_attn: float32 [2048], replicated, may hold values from 0.5 to 1.5
- norm_ffn: float32 [2048], replicated, may hold values from 0.5 to 1.5
- w_query: bfloat16 [2048, 2048], P(None, 'tensor'), may hold values from -0.125 to 0.125
- w_key: bfloat16 [2048, 2048], P(None, 'tensor'), may hold values from -0.125 to 0.125
- w_value: bfloat16 [2048, 2048], P(None, 'tensor'), may hold values from -0.125 to 0.125
- w_out: bfloat16 [2048, 2048], P('tensor'), may hold values from -0.5 to 0.5
- w_gate: bfloat16 [2048, 8192], P(None, 'tensor'), may hold values from -0.125 to 0.125
- w_up: bfloat16 [2048, 8192], P(None, 'tensor'), may hold values from -0.125 to 0.125
- w_down: bfloat16 [8192, 2048], P('tensor'), may hold values from -0.0625 to 0.0625
- doc_lengths: int32 [10], replicated, may hold values from 256 to 512, as said below
Outputs:
- block_output: bfloat16 [4096, 2048], P('dp', 'tensor')
- grad_input: bfloat16 [4096, 2048], P('dp', 'tensor')
- grad_norm_attn: float32 [2048], replicated
- grad_norm_ffn: float32 [2048], replicated
- grad_query: float32 [2048, 2048], P('dp', 'tensor')
- grad_key: float32 [2048, 2048], P('dp', 'tensor')
- grad_value: float32 [2048, 2048], P('dp', 'tensor')
- grad_out_proj: float32 [2048, 2048], P('tensor', 'dp')
- grad_gate: float32 [2048, 8192], P('dp', 'tensor')
- grad_up: float32 [2048, 8192], P('dp', 'tensor')
- grad_down: float32 [8192, 2048], P('tensor', 'dp')
Inputs may be any that keep to these rules, and one draw needn't show every extreme that they name: `doc_lengths`: every 2048 tokens in order form a row of exactly 5 whole documents; the first of each row has 512 tokens.
All inputs are finite; a program needn't handle non-finite values.
Results may differ from a plain program's by a relative error of at most 0.014.
Values may be sent and summed in bfloat16 or wider, within the bound.
A program may use at most 320 MiB of HBM per device.

v0:
```python
import jax
import jax.numpy as jnp
from jax import lax
from jax.sharding import PartitionSpec as P

HEAD_DIM = 64
ROW_LEN = 2048
BLK = 128
QBLK = 512
RECV = 1024
PEER = 512


EPS = 1e-05
THETA = 130000.0
MASKED = -1000000000.0


def assign_groups(doc_lengths, group_count):
    doc_count = doc_lengths.shape[0]
    doc_ids = jnp.arange(doc_count, dtype=jnp.int32)
    priority = (ROW_LEN - doc_lengths) * doc_count + doc_ids
    doc_rank = jnp.sum(
        (priority[None, :] < priority[:, None]).astype(jnp.int32), axis=1, dtype=jnp.int32
    )
    rounds = doc_rank // group_count
    within = doc_rank % group_count
    dealt = jnp.where(rounds % 2 == 0, within, group_count - 1 - within)
    return (dealt + 1) % group_count


def doc_tables(doc_lengths, doc_groups, group_id, token_count, capacity, block_pad):
    starts = jnp.cumsum(doc_lengths, dtype=jnp.int32) - doc_lengths
    padded = (doc_lengths + block_pad - 1) // block_pad * block_pad
    owned = doc_groups == group_id
    owned_pad = jnp.where(owned, padded, 0)
    rstart = jnp.cumsum(owned_pad, dtype=jnp.int32) - owned_pad
    buffer_pos = jnp.arange(capacity, dtype=jnp.int32)[:, None]
    inside = (
        owned[None, :]
        & (buffer_pos >= rstart[None, :])
        & (buffer_pos < rstart[None, :] + doc_lengths[None, :])
    )
    offsets = buffer_pos - rstart[None, :]
    filled = jnp.any(inside, axis=1)
    source = jnp.sum(jnp.where(inside, starts[None, :] + offsets, 0), axis=1, dtype=jnp.int32)
    position = jnp.sum(jnp.where(inside, offsets, 0), axis=1, dtype=jnp.int32)
    doc_ids = jnp.arange(doc_lengths.shape[0], dtype=jnp.int32)
    owner_doc = jnp.sum(jnp.where(inside, doc_ids[None, :], 0), axis=1, dtype=jnp.int32)
    segment = jnp.where(filled, owner_doc, -1 - buffer_pos[:, 0])
    token_ids = jnp.arange(token_count, dtype=jnp.int32)[:, None]
    belongs = (token_ids >= starts[None, :]) & (token_ids < starts[None, :] + doc_lengths[None, :])
    token_dest = jnp.sum(jnp.where(belongs, doc_groups[None, :], 0), axis=1, dtype=jnp.int32)
    back_pos = jnp.sum(
        jnp.where(belongs, rstart[None, :] + token_ids - starts[None, :], 0),
        axis=1,
        dtype=jnp.int32,
    )
    back_pos = jnp.clip(back_pos, 0, capacity - 1)
    return (filled, source, position, segment, token_dest, back_pos)


def rope_tables(position, head_dim):
    half_dim = head_dim // 2
    frequency = THETA ** (-jnp.arange(half_dim, dtype=jnp.float32) * 2.0 / head_dim)
    angles = position.astype(jnp.float32)[:, None] * frequency[None, :]
    return (jnp.cos(angles)[:, None, :], jnp.sin(angles)[:, None, :])


def rotate(values, cosine, sine, turn):
    half_dim = values.shape[-1] // 2
    front_half = values[..., :half_dim]
    back_half = values[..., half_dim:]
    return jnp.concatenate(
        [
            front_half * cosine - turn * back_half * sine,
            back_half * cosine + turn * front_half * sine,
        ],
        axis=-1,
    )


def times_rows(left, right):
    return lax.dot_general(
        left, right, (((0,), (0,)), ((), ())), preferred_element_type=jnp.float32
    )


def times_back(left, weight):
    return lax.dot_general(
        left, weight, (((1,), (1,)), ((), ())), preferred_element_type=jnp.float32
    )


def rms_scale(values):
    return lax.rsqrt(jnp.mean(values * values, axis=1, keepdims=True) + EPS)


def rms_back(values, scale, grad_normed, gain):
    weighted = grad_normed * gain
    return scale * (
        weighted - values * scale * scale * jnp.mean(weighted * values, axis=1, keepdims=True)
    )


def masked_scores(query_rows, key_low, segment, first_row):
    row_count = query_rows.shape[0]
    scores = jnp.einsum(
        "qhd,khd->hqk", query_rows, key_low, preferred_element_type=jnp.float32
    ) * query_rows.shape[-1] ** (-0.5)
    row_at = first_row + jnp.arange(row_count, dtype=jnp.int32)[:, None]
    col_at = jnp.arange(key_low.shape[0], dtype=jnp.int32)[None, :]
    row_seg = segment[first_row : first_row + row_count]
    allowed = (row_seg[:, None] == segment[None, :]) & (col_at <= row_at)
    return jnp.where(allowed[None], scores, MASKED)


def per_device(
    block_input,
    grad_output,
    norm_attn,
    norm_ffn,
    w_query,
    w_key,
    w_value,
    w_out,
    w_gate,
    w_up,
    w_down,
    doc_lengths,
):
    tok_dev = block_input.shape[0]
    width_part = block_input.shape[1]
    n_groups = lax.axis_size("dp")
    token_count = tok_dev * n_groups
    group_id = lax.axis_index("dp")
    shard_id = lax.axis_index("tensor")
    doc_groups = assign_groups(doc_lengths, n_groups)
    filled, source, position, segment, token_dest, back_pos = doc_tables(
        doc_lengths, doc_groups, group_id, token_count, RECV, BLK
    )
    local_dest = lax.dynamic_slice_in_dim(token_dest, group_id * tok_dev, tok_dev)
    zero_low = jnp.zeros((), jnp.bfloat16)
    keep_rows = filled[:, None]
    group_ids = jnp.arange(n_groups, dtype=jnp.int32)
    dest_view = token_dest.reshape(n_groups, tok_dev)
    hits = (dest_view[:, :, None] == group_ids[None, None, :]).astype(jnp.int32)
    ranks = jnp.cumsum(hits, axis=1, dtype=jnp.int32) - hits
    within = jnp.sum(ranks * hits, axis=2, dtype=jnp.int32)
    counts_to = jnp.sum(hits, axis=1, dtype=jnp.int32)
    within_flat = within.reshape(-1)
    my_within = lax.dynamic_slice_in_dim(within_flat, group_id * tok_dev, tok_dev)
    my_counts = lax.dynamic_index_in_dim(counts_to, group_id, 0, keepdims=False)
    slot_ids = jnp.arange(PEER, dtype=jnp.int32)
    send_at = local_dest * PEER + my_within
    send_table = (
        jnp.zeros((n_groups * PEER,), jnp.int32)
        .at[send_at]
        .set(jnp.arange(tok_dev, dtype=jnp.int32))
    )
    send_live = (slot_ids[None, :] < my_counts[:, None])[:, :, None]
    send_input = jnp.where(
        send_live, block_input[send_table].reshape(n_groups, PEER, width_part), zero_low
    )
    send_grad = jnp.where(
        send_live, grad_output[send_table].reshape(n_groups, PEER, width_part), zero_low
    )
    got_input, got_grad = (
        lax.all_to_all(send_input, "dp", split_axis=0, concat_axis=0, tiled=True),
        lax.all_to_all(send_grad, "dp", split_axis=0, concat_axis=0, tiled=True),
    )
    from_slot = source // tok_dev * PEER + within_flat[source]
    slot_input = jnp.where(
        keep_rows, got_input.reshape(n_groups * PEER, width_part)[from_slot], zero_low
    )
    slot_grad = jnp.where(
        keep_rows, got_grad.reshape(n_groups * PEER, width_part)[from_slot], zero_low
    )
    rows_low, grad_low = (
        lax.all_gather(slot_input, "tensor", axis=1, tiled=True),
        lax.all_gather(slot_grad, "tensor", axis=1, tiled=True),
    )
    rows_in = rows_low.astype(jnp.float32)
    scale_one = rms_scale(rows_in)
    normed_one = (rows_in * scale_one * norm_attn).astype(jnp.bfloat16)
    heads_local = w_query.shape[1] // HEAD_DIM
    cosine, sine = rope_tables(position, HEAD_DIM)
    query_f = jnp.dot(normed_one, w_query, preferred_element_type=jnp.float32).reshape(
        RECV, heads_local, HEAD_DIM
    )
    query_low = rotate(query_f, cosine, sine, 1.0).astype(jnp.bfloat16)
    key_f = jnp.dot(normed_one, w_key, preferred_element_type=jnp.float32).reshape(
        RECV, heads_local, HEAD_DIM
    )
    key_low = rotate(key_f, cosine, sine, 1.0).astype(jnp.bfloat16)
    value_low = (
        jnp.dot(normed_one, w_value, preferred_element_type=jnp.float32)
        .astype(jnp.bfloat16)
        .reshape(RECV, heads_local, HEAD_DIM)
    )
    attended_parts = []
    log_sums = []
    for block_number in range(RECV // QBLK):
        first_row = block_number * QBLK
        scores = masked_scores(query_low[first_row : first_row + QBLK], key_low, segment, first_row)
        row_peak = jnp.max(scores, axis=-1, keepdims=True)
        exponent = jnp.exp(scores - row_peak)
        row_mass = jnp.sum(exponent, axis=-1, keepdims=True)
        prob_low = (exponent / row_mass).astype(jnp.bfloat16)
        attended_parts.append(
            jnp.einsum("hqk,khd->qhd", prob_low, value_low, preferred_element_type=jnp.float32)
        )
        log_sums.append(row_peak + jnp.log(row_mass))
    attended = (
        jnp.concatenate(attended_parts, axis=0)
        .reshape(RECV, heads_local * HEAD_DIM)
        .astype(jnp.bfloat16)
    )
    attn_part = jnp.dot(attended, w_out, preferred_element_type=jnp.float32)
    hidden_state = rows_in + lax.psum(attn_part, "tensor")
    scale_two = rms_scale(hidden_state)
    normed_two = (hidden_state * scale_two * norm_ffn).astype(jnp.bfloat16)
    gate_proj = jnp.dot(normed_two, w_gate, preferred_element_type=jnp.float32)
    up_proj = jnp.dot(normed_two, w_up, preferred_element_type=jnp.float32)
    sigmoid_gate = jax.nn.sigmoid(gate_proj)
    inner = (gate_proj * sigmoid_gate * up_proj).astype(jnp.bfloat16)
    ffn_part = jnp.dot(inner, w_down, preferred_element_type=jnp.float32)
    ffn_full = lax.psum(ffn_part.astype(jnp.bfloat16), "tensor").astype(jnp.float32)
    out_slice = lax.dynamic_slice_in_dim(
        hidden_state + ffn_full, shard_id * width_part, width_part, 1
    )
    out_low = out_slice.astype(jnp.bfloat16)
    grad_rows = grad_low.astype(jnp.float32)
    grad_down = times_rows(inner, grad_low)
    d_inner = times_back(grad_low, w_down)
    d_gate = (d_inner * up_proj * sigmoid_gate * (1.0 + gate_proj * (1.0 - sigmoid_gate))).astype(
        jnp.bfloat16
    )
    d_up = (d_inner * gate_proj * sigmoid_gate).astype(jnp.bfloat16)
    grad_gate = times_rows(normed_two, d_gate)
    grad_up = times_rows(normed_two, d_up)
    d_normed_two = times_back(d_gate, w_gate) + times_back(d_up, w_up)
    gain_two = jnp.sum(d_normed_two * hidden_state * scale_two, axis=0)
    d_normed_two = lax.psum(d_normed_two, "tensor")
    d_hidden = grad_rows + rms_back(hidden_state, scale_two, d_normed_two, norm_ffn)
    d_hidden_low = d_hidden.astype(jnp.bfloat16)
    grad_wout = times_rows(attended, d_hidden_low)
    d_attended = (
        times_back(d_hidden_low, w_out).astype(jnp.bfloat16).reshape(RECV, heads_local, HEAD_DIM)
    )
    score_scale = HEAD_DIM ** (-0.5)
    d_query_parts = []
    d_key_rot = jnp.zeros((RECV, heads_local, HEAD_DIM), jnp.float32)
    d_value = jnp.zeros((RECV, heads_local, HEAD_DIM), jnp.float32)
    for block_number in range(RECV // QBLK):
        first_row = block_number * QBLK
        rows_query = query_low[first_row : first_row + QBLK]
        rows_grad = d_attended[first_row : first_row + QBLK]
        scores = masked_scores(rows_query, key_low, segment, first_row)
        prob = jnp.exp(scores - log_sums[block_number])
        prob_low = prob.astype(jnp.bfloat16)
        d_value = d_value + jnp.einsum(
            "hqk,qhd->khd", prob_low, rows_grad, preferred_element_type=jnp.float32
        )
        d_prob = jnp.einsum(
            "qhd,khd->hqk", rows_grad, value_low, preferred_element_type=jnp.float32
        )
        delta_row = jnp.sum(prob * d_prob, axis=-1, keepdims=True)
        d_scores = (prob * (d_prob - delta_row)).astype(jnp.bfloat16)
        d_query_parts.append(
            jnp.einsum("hqk,khd->qhd", d_scores, key_low, preferred_element_type=jnp.float32)
            * score_scale
        )
        d_key_rot = (
            d_key_rot
            + jnp.einsum("hqk,qhd->khd", d_scores, rows_query, preferred_element_type=jnp.float32)
            * score_scale
        )
    d_query = (
        rotate(jnp.concatenate(d_query_parts, axis=0), cosine, sine, -1.0)
        .astype(jnp.bfloat16)
        .reshape(RECV, heads_local * HEAD_DIM)
    )
    d_key = (
        rotate(d_key_rot, cosine, sine, -1.0)
        .astype(jnp.bfloat16)
        .reshape(RECV, heads_local * HEAD_DIM)
    )
    d_value_low = d_value.astype(jnp.bfloat16).reshape(RECV, heads_local * HEAD_DIM)
    grad_query = times_rows(normed_one, d_query)
    grad_key = times_rows(normed_one, d_key)
    grad_value = times_rows(normed_one, d_value_low)
    d_normed_one = (
        times_back(d_query, w_query) + times_back(d_key, w_key) + times_back(d_value_low, w_value)
    )
    gain_one = jnp.sum(d_normed_one * rows_in * scale_one, axis=0)
    d_normed_one = lax.psum(d_normed_one, "tensor")
    d_rows = d_hidden + rms_back(rows_in, scale_one, d_normed_one, norm_attn)
    d_rows_low = lax.dynamic_slice_in_dim(d_rows, shard_id * width_part, width_part, 1).astype(
        jnp.bfloat16
    )
    grad_query, grad_key, grad_value, grad_wout, grad_gate, grad_up, grad_down = (
        lax.psum_scatter(grad_query, "dp", scatter_dimension=0, tiled=True),
        lax.psum_scatter(grad_key, "dp", scatter_dimension=0, tiled=True),
        lax.psum_scatter(grad_value, "dp", scatter_dimension=0, tiled=True),
        lax.psum_scatter(grad_wout, "dp", scatter_dimension=1, tiled=True),
        lax.psum_scatter(grad_gate, "dp", scatter_dimension=0, tiled=True),
        lax.psum_scatter(grad_up, "dp", scatter_dimension=0, tiled=True),
        lax.psum_scatter(grad_down, "dp", scatter_dimension=1, tiled=True),
    )
    gain_one, gain_two = lax.psum((gain_one, gain_two), ("dp", "tensor"))
    token_all = jnp.arange(token_count, dtype=jnp.int32)
    return_at = jnp.where(
        token_dest == group_id, token_all // tok_dev * PEER + within_flat, n_groups * PEER
    )
    return_table = (
        jnp.zeros((n_groups * PEER + 1,), jnp.int32).at[return_at].set(back_pos)[: n_groups * PEER]
    )
    from_counts = lax.dynamic_index_in_dim(counts_to, group_id, 1, keepdims=False)
    return_live = (slot_ids[None, :] < from_counts[:, None])[:, :, None]
    send_out = jnp.where(
        return_live, out_low[return_table].reshape(n_groups, PEER, width_part), zero_low
    )
    send_back = jnp.where(
        return_live, d_rows_low[return_table].reshape(n_groups, PEER, width_part), zero_low
    )
    back_out, back_grad = (
        lax.all_to_all(send_out, "dp", split_axis=0, concat_axis=0, tiled=True),
        lax.all_to_all(send_back, "dp", split_axis=0, concat_axis=0, tiled=True),
    )
    rows_from = local_dest * PEER + my_within
    block_output = back_out.reshape(n_groups * PEER, width_part)[rows_from]
    grad_input = back_grad.reshape(n_groups * PEER, width_part)[rows_from]
    return (
        block_output,
        grad_input,
        gain_one,
        gain_two,
        grad_query,
        grad_key,
        grad_value,
        grad_wout,
        grad_gate,
        grad_up,
        grad_down,
    )


def solution(mesh):
    return jax.shard_map(
        per_device,
        mesh=mesh,
        in_specs=(
            P("dp", "tensor"),
            P("dp", "tensor"),
            P(),
            P(),
            P(None, "tensor"),
            P(None, "tensor"),
            P(None, "tensor"),
            P("tensor", None),
            P(None, "tensor"),
            P(None, "tensor"),
            P("tensor", None),
            P(),
        ),
        out_specs=(
            P("dp", "tensor"),
            P("dp", "tensor"),
            P(),
            P(),
            P("dp", "tensor"),
            P("dp", "tensor"),
            P("dp", "tensor"),
            P("tensor", "dp"),
            P("dp", "tensor"),
            P("dp", "tensor"),
            P("tensor", "dp"),
        ),
        check_vma=False,
    )
```

profile of v0, /device:TPU:0, one launch (start us, length us, event | category | flops | bytes accessed | tf_op | source)
XLA Modules:
  0.0 2384.8 jit_solution(11213583537056394116)
XLA Ops:
  11.4 9.0 reduce-window.30
  23.9 17.3 gather_fusion.5
  41.3 17.3 gather_fusion
  63.7 100.3 %all_to_all.20 = bf16[8,512,512]{2,1,0:T(8,128)(2,1)} all-to-all(bf16[8,512,512]{2,1,0:T(8,128)(2,1)S(1)} %get-tuple-element.55), channel_id=1, replica_groups=mesh['dp'=8,'tensor'=4] {'dp'}, dimensions={0} | all-to-all | bytes 8388608 | tf_op jit(solution)/shard_map/all_to_all | solution.py:170
  175.1 6.7 gather_fusion.6
  181.9 79.1 %all-to-all-done = bf16[8,512,512]{2,1,0:T(8,128)(2,1)} async-done(((bf16[8,512,512]{2,1,0:T(8,128)(2,1)}), bf16[8,512,512]{2,1,0:T(8,128)(2,1)}, u32[]{:S(2)}, u32[]{:S(2)}) %all-to-all-start) | async-done | bytes 4194336 | tf_op jit(solution)/shard_map/all_to_all | solution.py:169
  260.9 7.9 gather_fusion.2
  274.2 31.0 %all-gather.3.cloned.1.call-done = bf16[1024,2048]{1,0:T(8,128)(2,1)} async-done(((bf16[1024,512]{1,0:T(8,128)(2,1)}), bf16[1024,2048]{1,0:T(8,128)(2,1)}) %all-gather.3.cloned.1.call-update) | async-done | bytes 4194320 | tf_op jit(solution)/shard_map/all_gather | solution.py:180
  320.4 7.9 fusion.73
  338.5 7.7 fusion
  346.2 7.5 fusion.35
  361.3 152.2 %all-reduce.6.cloned.1.call-done = f32[1024,2048]{1,0:T(8,128)} async-done(((f32[1024,2048]{1,0:T(8,128)}), f32[1024,2048]{1,0:T(8,128)}) %all-reduce.6.cloned.1.call-update) | async-done | bytes 8388624 | tf_op jit(solution)/shard_map/psum | solution.py:220
  520.0 17.0 fusion.76
  537.0 13.3 fusion.75
  550.3 21.8 multiply_convert_fusion.2
  572.1 12.9 fusion.77
  585.0 13.5 convolution_add_fusion
  599.2 13.9 convolution_convert_fusion
  613.1 138.4 %all-reduce.10.cloned.1.call-done = f32[1024,2048]{1,0:T(8,128)} async-done(((f32[1024,2048]{1,0:T(8,128)}), f32[1024,2048]{1,0:T(8,128)}) %all-reduce.10.cloned.1.call-update) | async-done | bytes 8388624 | tf_op jit(solution)/shard_map/psum | solution.py:244
  751.6 11.1 multiply_reduce_fusion.2
  762.7 10.0 multiply_add_fusion
  772.7 6.7 fusion.28
  780.3 9.5 multiply_reduce_fusion.1
  789.8 16.1 multiply_convert_fusion.1
  806.0 8.1 fusion.32
  823.3 10.4 multiply_reduce_fusion
  833.7 10.3 multiply_convert_fusion
  853.7 6.7 fusion.78
  869.4 12.1 add_add_fusion
  882.7 7.6 fusion.20
  890.4 6.9 fusion.64
  897.4 7.1 fusion.65
  904.8 6.9 fusion.66
  911.8 15.2 fusion.82
  927.0 15.2 fusion.81
  942.6 15.3 fusion.80
  958.9 15.5 scatter_custom_fusion.1
  976.7 17.3 gather_fusion.3
  994.1 40.2 %all-reduce.12.cloned.1.call-done = f32[1024,2048]{1,0:T(8,128)} async-done(((f32[1024,2048]{1,0:T(8,128)}), f32[1024,2048]{1,0:T(8,128)}) %all-reduce.12.cloned.1.call-update) | async-done | bytes 8388624 | tf_op jit(solution)/shard_map/psum | solution.py:297
  1034.3 11.8 fusion.11
  1048.9 17.3 gather_fusion.7
  1071.5 129.8 %all_to_all.21 = bf16[8,512,512]{2,1,0:T(8,128)(2,1)} all-to-all(bf16[8,512,512]{2,1,0:T(8,128)(2,1)S(1)} %get-tuple-element.53), channel_id=1, replica_groups=mesh['dp'=8,'tensor'=4] {'dp'}, dimensions={0} | all-to-all | bytes 8388608 | tf_op jit(solution)/shard_map/all_to_all | solution.py:329
  1206.0 128.8 %all-reduce = (f32[2048]{0:T(1024)}, f32[2048]{0:T(1024)}) all-reduce(f32[2048]{0:T(1024)S(1)} %get-tuple-element.13, f32[2048]{0:T(1024)S(1)} %copy-done.44), channel_id=1, replica_groups=mesh['dp'=8,'tensor'=4] {'dp','tensor'}, use_global_device_ids=true, to_apply=%region_30.31 | all-reduce | flops 4096 | bytes 32768 | tf_op jit(solution)/shard_map/psum | solution.py:311
  1345.6 80.5 %reduce-scatter.10.cloned.1.call-done = f32[256,512]{1,0:T(8,128)} async-done(((f32[2048,512]{1,0:T(8,128)}), f32[256,512]{1,0:T(8,128)}) %reduce-scatter.10.cloned.1.call-update) | async-done | bytes 524304 | tf_op jit(solution)/shard_map/reduce_scatter | solution.py:304
  1426.1 91.7 %reduce-scatter.8.cloned.1.call-done = f32[256,512]{1,0:T(8,128)} async-done(((f32[2048,512]{1,0:T(8,128)}), f32[256,512]{1,0:T(8,128)}) %reduce-scatter.8.cloned.1.call-update) | async-done | bytes 524304 | tf_op jit(solution)/shard_map/reduce_scatter | solution.py:303
  1517.8 287.4 %reduce-scatter.20.cloned.1.call-done = f32[2048,256]{1,0:T(8,128)} async-done(((f32[2048,2048]{1,0:T(8,128)}), f32[2048,256]{1,0:T(8,128)}) %reduce-scatter.20.cloned.1.call-update) | async-done | bytes 2097168 | tf_op jit(solution)/shard_map/reduce_scatter | solution.py:309
  1805.2 285.9 %reduce-scatter.18.cloned.1.call-done = f32[256,2048]{1,0:T(8,128)} async-done(((f32[2048,2048]{1,0:T(8,128)}), f32[256,2048]{1,0:T(8,128)}) %reduce-scatter.18.cloned.1.call-update) | async-done | bytes 2097168 | tf_op jit(solution)/shard_map/reduce_scatter | solution.py:308
  2091.2 286.6 %reduce-scatter.16.cloned.1.call-done = f32[256,2048]{1,0:T(8,128)} async-done(((f32[2048,2048]{1,0:T(8,128)}), f32[256,2048]{1,0:T(8,128)}) %reduce-scatter.16.cloned.1.call-update) | async-done | bytes 2097168 | tf_op jit(solution)/shard_map/reduce_scatter | solution.py:307
  (248 shorter events, 126.5 us)
Async XLA Ops:
  7.2 347.7 %copy-start = (bf16[512,2048]{1,0:T(8,128)(2,1)S(1)}, bf16[512,2048]{1,0:T(8,128)(2,1)}, u32[]{:S(2)}) copy-start(bf16[512,2048]{1,0:T(8,128)(2,1)} %param.19) | copy-start | bytes 6291460
  7.2 16.7 copy-start.2
  11.4 12.5 copy-start.35
  23.9 17.4 copy-start.3
  164.0 96.9 %all-to-all-start = ((bf16[8,512,512]{2,1,0:T(8,128)(2,1)}), bf16[8,512,512]{2,1,0:T(8,128)(2,1)}, u32[]{:S(2)}, u32[]{:S(2)}) async-start(bf16[8,512,512]{2,1,0:T(8,128)(2,1)} %get-tuple-element.56), calls=%async_computation | async-start | bytes 8388608 | tf_op jit(solution)/shard_map/all_to_all | solution.py:169
  168.6 136.7 %all-gather.3.cloned.1.call-start = ((), (), s32[]{:S(2)}) async-start(), calls=%async_computation.11 | async-start | bytes 5242880 | tf_op jit(solution)/shard_map/all_gather | solution.py:180
  260.9 47.4 %copy-start.47 = (f32[2048]{0:T(1024)S(1)}, f32[2048]{0:T(1024)}, u32[]{:S(2)}) copy-start(f32[2048]{0:T(1024)} %param.14) | copy-start | bytes 24580
  271.6 241.9 %all-reduce.6.cloned.1.call-start = ((), (), s32[]{:S(2)}) async-start(), calls=%async_computation.12 | async-start | bytes 16777216 | tf_op jit(solution)/shard_map/psum | solution.py:220
  272.9 43.6 %copy-start.26 = (f32[1024,32]{0,1:T(8,128)}, f32[1024,32]{0,1:T(8,128)S(1)}, u32[]{:S(2)}) copy-start(f32[1024,32]{0,1:T(8,128)S(1)} %get-tuple-element.52) | copy-start | bytes 393220
  308.4 23.7 copy-start.42
  320.4 14.3 copy-start.4
  334.7 11.5 copy-start.23
  360.5 189.8 %all-gather.5.cloned.1.call-start = ((), (), s32[]{:S(2)}) async-start(), calls=%async_computation.14 | async-start | bytes 5242880 | tf_op jit(solution)/shard_map/all_gather | solution.py:181
  361.2 158.0 %copy-start.40 = (f32[2048]{0:T(1024)S(1)}, f32[2048]{0:T(1024)}, u32[]{:S(2)}) copy-start(f32[2048]{0:T(1024)} %param.15) | copy-start | bytes 24580
  361.2 390.3 %all-reduce.10.cloned.1.call-start = ((), (), s32[]{:S(2)}) async-start(), calls=%async_computation.15 | async-start | bytes 16777216 | tf_op jit(solution)/shard_map/psum | solution.py:244
  519.2 17.8 copy-start.5
  520.0 17.0 copy-start.21
  572.1 12.9 copy-start.54
  598.5 376.0 %all-reduce.8.cloned.1.call-start = ((), (), s32[]{:S(2)}) async-start(), calls=%async_computation.13 | async-start | bytes 8388608 | tf_op jit(solution)/shard_map/psum | solution.py:228
  613.1 421.2 %all-reduce.12.cloned.1.call-start = ((), (), s32[]{:S(2)}) async-start(), calls=%async_computation.16 | async-start | bytes 16777216 | tf_op jit(solution)/shard_map/psum | solution.py:297
  751.6 11.1 copy-start.22
  762.7 17.6 slice-start.4
  762.7 17.6 slice-start.5
  762.7 17.6 slice-start.6
  780.3 9.5 copy-start.18
  789.8 16.2 copy-start.14
  789.8 16.2 copy-start.16
  789.8 29.4 %slice-start = ((s8[16777216]{0:T(1024)(128)(4,1)}), s8[4194304]{0:T(1024)(128)(4,1)S(1)}, s32[]{:S(2)}) async-start(s8[16777216]{0:T(1024)(128)(4,1)} %bitcast.107), calls=%async_computation.24 | async-start | bytes 8388608
  789.8 29.4 %slice-start.1 = ((s8[16777216]{0:T(1024)(128)(4,1)}), s8[4194304]{0:T(1024)(128)(4,1)S(1)}, s32[]{:S(2)}) async-start(s8[16777216]{0:T(1024)(128)(4,1)} %bitcast.107), calls=%async_computation.25 | async-start | bytes 8388608
  789.8 29.4 %slice-start.2 = ((s8[16777216]{0:T(1024)(128)(4,1)}), s8[4194304]{0:T(1024)(128)(4,1)S(1)}, s32[]{:S(2)}) async-start(s8[16777216]{0:T(1024)(128)(4,1)} %bitcast.107), calls=%async_computation.26 | async-start | bytes 8388608
  806.0 8.1 copy-start.9
  806.0 13.2 slice-start.3
  852.2 14.0 slice-start.8
  852.9 13.2 slice-start.9
  853.7 12.4 slice-start.10
  881.5 8.9 copy-start.43
  881.5 8.9 copy-start.48
  881.5 464.1 %reduce-scatter.14.cloned.1.call-start = ((), (), s32[]{:S(2)}) async-start(), calls=%async_computation.20 | async-start | bytes 4718592 | tf_op jit(solution)/shard_map/reduce_scatter | solution.py:306
  890.3 455.3 %reduce-scatter.12.cloned.1.call-start = ((), (), s32[]{:S(2)}) async-start(), calls=%async_computation.19 | async-start | bytes 4718592 | tf_op jit(solution)/shard_map/reduce_scatter | solution.py:305
  897.4 528.8 %reduce-scatter.10.cloned.1.call-start = ((), (), s32[]{:S(2)}) async-start(), calls=%async_computation.18 | async-start | bytes 4718592 | tf_op jit(solution)/shard_map/reduce_scatter | solution.py:304
  904.6 613.3 %reduce-scatter.8.cloned.1.call-start = ((), (), s32[]{:S(2)}) async-start(), calls=%async_computation.17 | async-start | bytes 4718592 | tf_op jit(solution)/shard_map/reduce_scatter | solution.py:303
  911.7 893.5 %reduce-scatter.20.cloned.1.call-start = ((), (), s32[]{:S(2)}) async-start(), calls=%async_computation.23 | async-start | bytes 18874368 | tf_op jit(solution)/shard_map/reduce_scatter | solution.py:309
  927.0 1164.2 %reduce-scatter.18.cloned.1.call-start = ((), (), s32[]{:S(2)}) async-start(), calls=%async_computation.22 | async-start | bytes 18874368 | tf_op jit(solution)/shard_map/reduce_scatter | solution.py:308
  942.3 1435.5 %reduce-scatter.16.cloned.1.call-start = ((), (), s32[]{:S(2)}) async-start(), calls=%async_computation.21 | async-start | bytes 18874368 | tf_op jit(solution)/shard_map/reduce_scatter | solution.py:307
  1071.5 134.5 %copy-start.50 = (s32[512]{0:T(512)S(1)}, s32[512]{0:T(512)}, u32[]{:S(2)}) copy-start(s32[512]{0:T(512)} %copy-done.49) | copy-start | bytes 6148
  1071.5 134.5 %copy-start.44 = (f32[2048]{0:T(1024)S(1)}, f32[2048]{0:T(1024)}, u32[]{:S(2)}) copy-start(f32[2048]{0:T(1024)} %get-tuple-element.11) | copy-start | bytes 24580
  1201.3 1176.4 %copy-start.1 = (bf16[512,2048]{1,0:T(8,128)(2,1)S(1)}, bf16[512,2048]{1,0:T(8,128)(2,1)}, u32[]{:S(2)}) copy-start(bf16[512,2048]{1,0:T(8,128)(2,1)} %param.19) | copy-start | bytes 6291460
  1201.3 138.9 %all-to-all-start.1 = ((bf16[8,512,512]{2,1,0:T(8,128)(2,1)}), bf16[8,512,512]{2,1,0:T(8,128)(2,1)}, u32[]{:S(2)}, u32[]{:S(2)}) async-start(bf16[8,512,512]{2,1,0:T(8,128)(2,1)} %get-tuple-element.54), calls=%async_computation.1 | async-start | bytes 8388608 | tf_op jit(solution)/shard_map/all_to_all | solution.py:328
  (34 other events, 140.2 us)
Sparse Core Ops, SparseCore 0:
  271.7 33.5 all-gather.2
  360.6 152.8 all-reduce.5
  515.6 34.6 all-gather.4
  598.6 152.9 all-reduce.9
  753.8 85.6 all-reduce.7
  881.6 152.6 all-reduce.11
  1038.9 133.5 reduce-scatter.13
  1176.7 157.0 reduce-scatter.11
  1338.5 87.5 reduce-scatter.9
  1430.2 87.6 reduce-scatter.7
  1522.7 282.4 reduce-scatter.19
  1809.4 281.6 reduce-scatter.17
  2096.0 281.6 reduce-scatter.15
where the time goes:
time: 2390 us; the launch traced here: 2380 us
  waiting for transfers between devices  1470 us (62%)
  blocking collectives  359 us (15%)
  matrix products  285 us (12%)
  local copies, waits for them, and re-layouts  124 us (5%)
  other arithmetic  118 us (5%)
    reduce_scatter x1, waiting for transfers between devices, per_device(): lax.psum_scatter(grad_down, 'dp', scatter_dimension=1, tiled=True)  287 us
    reduce_scatter x1, waiting for transfers between devices, per_device(): lax.psum_scatter(grad_gate, 'dp', scatter_dimension=0, tiled=True)  287 us
    reduce_scatter x1, waiting for transfers between devices, per_device(): lax.psum_scatter(grad_up, 'dp', scatter_dimension=0, tiled=True)  286 us
    psum x1, waiting for transfers between devices, per_device(): hidden_state = rows_in + lax.psum(attn_part, 'tensor')  152 us
    psum x1, waiting for transfers between devices, per_device(): d_normed_two = lax.psum(d_normed_two, 'tensor')  138 us
    all_to_all x1, blocking collectives, per_device(): lax.all_to_all(send_back, 'dp', split_axis=0, concat_axis=0, tiled=True)  130 us
    psum x1, blocking collectives, per_device(): gain_one, gain_two = lax.psum((gain_one, gain_two), ('dp', 'tensor'))  129 us
    all_to_all x1, blocking collectives, per_device(): lax.all_to_all(send_grad, 'dp', split_axis=0, concat_axis=0, tiled=True)  100 us
  transfers between devices with their start and end apart: 15, of which 10 were waited for; matrix products, arithmetic and copies ran while one was open for 15% of the time, Pallas kernels for 0%

commit v1 on v0

v1 whole, which is shorter than its diff:
```python
import jax
import jax.numpy as jnp
from jax import lax
from jax.sharding import PartitionSpec as P

HEAD_DIM = 64
ROW_LEN = 2048
EPS = 1e-05
THETA = 130000.0
MASKED = -1000000000.0
RING = 4

F32 = jnp.float32
LOW = jnp.bfloat16


def mm(left, right, lc, rc):
    return lax.dot_general(left, right, (((lc,), (rc,)), ((), ())), preferred_element_type=F32)


def bits_of(size):
    step = size // 2
    while step:
        yield step
        step //= 2


def swap(values, axis, mask):
    count = lax.axis_size(axis)
    return lax.ppermute(values, axis, [(i, i ^ mask) for i in range(count)])


def sum_all(values, axis, masks):
    for mask in masks:
        values = values + swap(values, axis, mask)
    return values


def gather_features(part):
    count = lax.axis_size("tensor")
    me = lax.axis_index("tensor")
    rows, width = part.shape
    held = {0: part}
    for mask in bits_of(count):
        held.update({mask | at: swap(block, "tensor", mask) for at, block in list(held.items())})
    whole = jnp.zeros((rows, count * width), part.dtype)
    for at, block in held.items():
        whole = lax.dynamic_update_slice(whole, block, (0, (me ^ at) * width))
    return whole


def scatter_features(product):
    count = lax.axis_size("tensor")
    me = lax.axis_index("tensor")
    core = me % 2
    chip = me // 2
    sent = product(1 - core).astype(LOW)
    got = swap(sent, "tensor", 1)
    kept = product(core) + got.astype(F32)
    chips = count // 2
    width = kept.shape[1] // chips
    total = None
    for mask in range(1, chips):
        other = lax.dynamic_slice_in_dim(kept, (chip ^ mask) * width, width, 1).astype(LOW)
        come = swap(other, "tensor", mask * 2).astype(F32)
        total = come if total is None else total + come
    mine = lax.dynamic_slice_in_dim(kept, chip * width, width, 1)
    return mine if total is None else mine + total


def core_columns(weight, core):
    count = lax.axis_size("tensor")
    rows, cols = weight.shape
    view = weight.reshape(rows, count // 2, 2, cols // count)
    return lax.dynamic_index_in_dim(view, core, 2, False).reshape(rows, cols // 2)


def core_rows(weight, core):
    count = lax.axis_size("tensor")
    rows, cols = weight.shape
    view = weight.reshape(count // 2, 2, rows // count, cols)
    return lax.dynamic_index_in_dim(view, core, 1, False).reshape(rows // 2, cols)


def rope_tables(position):
    half_dim = HEAD_DIM // 2
    frequency = THETA ** (-jnp.arange(half_dim, dtype=F32) * 2.0 / HEAD_DIM)
    angles = position.astype(F32)[:, None] * frequency[None, :]
    return (jnp.cos(angles)[:, None, :], jnp.sin(angles)[:, None, :])


def rotate(values, cosine, sine, turn):
    half_dim = values.shape[-1] // 2
    front_half = values[..., :half_dim]
    back_half = values[..., half_dim:]
    return jnp.concatenate(
        [
            front_half * cosine - turn * back_half * sine,
            back_half * cosine + turn * front_half * sine,
        ],
        axis=-1,
    )


def per_device(
    block_input,
    grad_output,
    norm_attn,
    norm_ffn,
    w_query,
    w_key,
    w_value,
    w_out,
    w_gate,
    w_up,
    w_down,
    doc_lengths,
):
    tok, width = block_input.shape
    width_all = norm_attn.shape[0]
    n_dp = lax.axis_size("dp")
    me = lax.axis_index("dp")
    shard = lax.axis_index("tensor")
    ring = min(RING, n_dp // 2)
    blocks = n_dp // (2 * ring)
    pair_at = me % 2
    ring_at = (me // 2) % ring
    block_at = me // (2 * ring)
    owned = width_all // n_dp

    def ring_step(values):
        pairs = []
        for i in range(n_dp):
            b, k, c = i // (2 * ring), (i // 2) % ring, i % 2
            pairs.append((i, (b * ring + (k + 1) % ring) * 2 + c))
        return lax.ppermute(values, "dp", pairs)

    row_groups = ROW_LEN // tok
    halo_pairs = [
        (i, i + 1) for i in range(n_dp) if 0 < i % row_groups < row_groups - 1
    ]
    back_pairs = [(j, i) for i, j in halo_pairs]

    starts = jnp.cumsum(doc_lengths, dtype=jnp.int32) - doc_lengths
    token_ids = me * tok + jnp.arange(tok, dtype=jnp.int32)
    doc_start = jnp.max(
        jnp.where(starts[None, :] <= token_ids[:, None], starts[None, :], 0), axis=1
    )
    position = token_ids - doc_start
    cosine, sine = rope_tables(position)

    my_gain_one = lax.dynamic_slice_in_dim(norm_attn, shard * width, width)
    my_gain_two = lax.dynamic_slice_in_dim(norm_ffn, shard * width, width)

    rows_low = gather_features(block_input)
    rows_in = rows_low.astype(F32)
    scale_one = lax.rsqrt(jnp.mean(rows_in * rows_in, axis=1, keepdims=True) + EPS)
    normed_one = (rows_in * scale_one * norm_attn).astype(LOW)
    my_rows = block_input.astype(F32)
    my_grad = grad_output.astype(F32)

    grad_low = gather_features(grad_output)

    heads = w_query.shape[1] // HEAD_DIM
    key_f = mm(normed_one, w_key, 1, 0).reshape(tok, heads, HEAD_DIM)
    key_low = rotate(key_f, cosine, sine, 1.0).astype(LOW)
    value_low = mm(normed_one, w_value, 1, 0).astype(LOW).reshape(tok, heads, HEAD_DIM)
    halo_key = lax.ppermute(key_low, "dp", halo_pairs)
    halo_value = lax.ppermute(value_low, "dp", halo_pairs)
    query_f = mm(normed_one, w_query, 1, 0).reshape(tok, heads, HEAD_DIM)
    query_low = rotate(query_f, cosine, sine, 1.0).astype(LOW)

    score_scale = HEAD_DIM ** (-0.5)
    keys = jnp.concatenate([halo_key, key_low], axis=0)
    values = jnp.concatenate([halo_value, value_low], axis=0)
    key_ids = (me - 1) * tok + jnp.arange(2 * tok, dtype=jnp.int32)
    allowed = (key_ids[None, :] >= doc_start[:, None]) & (key_ids[None, :] <= token_ids[:, None])
    scores = jnp.einsum("qhd,khd->hqk", query_low, keys, preferred_element_type=F32) * score_scale
    scores = jnp.where(allowed[None], scores, MASKED)
    peak = jnp.max(scores, axis=-1, keepdims=True)
    exponent = jnp.exp(scores - peak)
    mass = jnp.sum(exponent, axis=-1, keepdims=True)
    prob_low = (exponent / mass).astype(LOW)
    log_sum = peak + jnp.log(mass)
    attended = (
        jnp.einsum("hqk,khd->qhd", prob_low, values, preferred_element_type=F32)
        .reshape(tok, heads * HEAD_DIM)
        .astype(LOW)
    )

    hidden = my_rows + scatter_features(lambda core: mm(attended, core_columns(w_out, core), 1, 0))
    tensor_masks = [1 << i for i in range((lax.axis_size("tensor") - 1).bit_length())]
    square = sum_all(jnp.sum(hidden * hidden, axis=1), "tensor", tensor_masks)
    scale_two = lax.rsqrt(square / width_all + EPS)[:, None]
    normed_slice = (hidden * scale_two * my_gain_two).astype(LOW)
    normed_two = gather_features(normed_slice)

    gate = mm(normed_two, w_gate, 1, 0)
    up = mm(normed_two, w_up, 1, 0)
    sig = jax.nn.sigmoid(gate)
    inner = (gate * sig * up).astype(LOW)
    ffn = scatter_features(lambda core: mm(inner, core_columns(w_down, core), 1, 0))
    block_output = (hidden + ffn).astype(LOW)

    def ffn_back(gate, up, sig, grads):
        d_inner = mm(grads, w_down, 1, 1)
        d_gate = (d_inner * up * sig * (1.0 + gate * (1.0 - sig))).astype(LOW)
        d_up = (d_inner * gate * sig).astype(LOW)
        return d_gate, d_up

    d_gate, d_up = ffn_back(gate, up, sig, grad_low)
    d_normed_two = scatter_features(
        lambda core: mm(d_gate, core_rows(w_gate, core), 1, 1)
        + mm(d_up, core_rows(w_up, core), 1, 1)
    )
    gain_two = jnp.sum(d_normed_two * hidden * scale_two, axis=0)
    weighted = d_normed_two * my_gain_two
    mean_two = sum_all(jnp.sum(weighted * hidden, axis=1), "tensor", tensor_masks) / width_all
    d_hidden = my_grad + scale_two * (
        weighted - hidden * scale_two * scale_two * mean_two[:, None]
    )
    d_hidden_low = gather_features(d_hidden.astype(LOW))

    normed_parts, grad_parts = [], []
    normed_at, grad_at = normed_slice, grad_output
    for _ in range(ring - 1):
        grad_at = ring_step(grad_at)
        grad_parts.append(gather_features(grad_at))
    for _ in range(ring - 1):
        normed_at = ring_step(normed_at)
        normed_parts.append(gather_features(normed_at))
    far_normed = jnp.concatenate(normed_parts, axis=0)
    far_grad = jnp.concatenate(grad_parts, axis=0)
    far_gate = mm(far_normed, w_gate, 1, 0)
    far_up = mm(far_normed, w_up, 1, 0)
    far_sig = jax.nn.sigmoid(far_gate)
    far_inner = (far_gate * far_sig * far_up).astype(LOW)
    far_d_gate, far_d_up = ffn_back(far_gate, far_up, far_sig, far_grad)

    def owned_columns(rows, at):
        view = rows.reshape(rows.shape[0], blocks, ring, 2, owned)
        view = lax.dynamic_index_in_dim(view, at // 2, 1, False)
        view = lax.dynamic_index_in_dim(view, ring_at, 1, False)
        return lax.dynamic_index_in_dim(view, at % 2, 1, False)

    seat = block_at * 2 + pair_at
    seats = blocks * 2

    def seat_swap(values, mask):
        pairs = []
        for i in range(n_dp):
            b, k, c = i // (2 * ring), (i // 2) % ring, i % 2
            s = (b * 2 + c) ^ mask
            pairs.append((i, ((s // 2) * ring + k) * 2 + s % 2))
        return lax.ppermute(values, "dp", pairs)

    def ffn_weight_grad(near_rows, far_rows, near_units, far_units, units_first):
        def part(at):
            near = owned_columns(near_rows, at)
            far = owned_columns(far_rows, at)
            if units_first:
                return mm(far_units, far, 0, 0) + mm(near_units, near, 0, 0)
            return mm(far, far_units, 0, 0) + mm(near, near_units, 0, 0)

        come = [
            seat_swap(part(seat ^ mask).astype(LOW), mask) for mask in range(1, seats)
        ]
        total = part(seat)
        for value in come:
            total = total + value.astype(F32)
        return total

    grad_down = ffn_weight_grad(grad_low, far_grad, inner, far_inner, True)
    grad_gate = ffn_weight_grad(normed_two, far_normed, d_gate, far_d_gate, False)
    grad_up = ffn_weight_grad(normed_two, far_normed, d_up, far_d_up, False)

    d_attended = mm(d_hidden_low, w_out, 1, 1).astype(LOW).reshape(tok, heads, HEAD_DIM)
    scores = jnp.einsum("qhd,khd->hqk", query_low, keys, preferred_element_type=F32) * score_scale
    scores = jnp.where(allowed[None], scores, MASKED)
    prob = jnp.exp(scores - log_sum)
    d_values = jnp.einsum("hqk,qhd->khd", prob.astype(LOW), d_attended, preferred_element_type=F32)
    d_prob = jnp.einsum("qhd,khd->hqk", d_attended, values, preferred_element_type=F32)
    delta = jnp.sum(prob * d_prob, axis=-1, keepdims=True)
    d_scores = (prob * (d_prob - delta)).astype(LOW)
    d_query_rot = (
        jnp.einsum("hqk,khd->qhd", d_scores, keys, preferred_element_type=F32) * score_scale
    )
    d_keys_rot = (
        jnp.einsum("hqk,qhd->khd", d_scores, query_low, preferred_element_type=F32) * score_scale
    )
    back_key = lax.ppermute(d_keys_rot[:tok].astype(LOW), "dp", back_pairs)
    back_value = lax.ppermute(d_values[:tok].astype(LOW), "dp", back_pairs)
    d_key_rot = d_keys_rot[tok:] + back_key.astype(F32)
    d_value_f = d_values[tok:] + back_value.astype(F32)
    flat = (tok, heads * HEAD_DIM)
    d_query = rotate(d_query_rot, cosine, sine, -1.0).astype(LOW).reshape(flat)
    d_key = rotate(d_key_rot, cosine, sine, -1.0).astype(LOW).reshape(flat)
    d_value = d_value_f.astype(LOW).reshape(flat)

    d_normed_one = scatter_features(
        lambda core: mm(d_query, core_rows(w_query, core), 1, 1)
        + mm(d_key, core_rows(w_key, core), 1, 1)
        + mm(d_value, core_rows(w_value, core), 1, 1)
    )
    gain_one = jnp.sum(d_normed_one * my_rows * scale_one, axis=0)
    weighted = d_normed_one * my_gain_one
    mean_one = sum_all(jnp.sum(weighted * my_rows, axis=1), "tensor", tensor_masks) / width_all
    d_rows = d_hidden + scale_one * (
        weighted - my_rows * scale_one * scale_one * mean_one[:, None]
    )
    grad_input = d_rows.astype(LOW)

    def attn_weight_grad(rows, units, units_first):
        pieces = rows.reshape(tok, blocks, ring, 2, owned)

        def part(at):
            mine = lax.dynamic_index_in_dim(pieces, at, 3, False).reshape(tok, -1)
            return mm(units, mine, 0, 0) if units_first else mm(mine, units, 0, 0)

        def split(values):
            if units_first:
                return values.reshape(-1, blocks, ring, owned)
            return values.reshape(blocks, ring, owned, -1)

        axis = 2 if units_first else 1
        come = swap(part(1 - pair_at).astype(LOW), "dp", 1)
        total = split(part(pair_at) + come.astype(F32))
        moving = None
        for step in range(1, ring + 1):
            at = (ring_at - step) % ring
            term = lax.dynamic_index_in_dim(total, at, axis, False)
            moving = term if moving is None else moving.astype(F32) + term
            if step < ring:
                moving = ring_step(moving.astype(LOW))
        axis = 1 if units_first else 0
        mine = lax.dynamic_index_in_dim(moving, block_at, axis, False)
        for mask in range(1, blocks):
            other = lax.dynamic_index_in_dim(moving, block_at ^ mask, axis, False)
            come = swap(other.astype(LOW), "dp", mask * 2 * ring)
            mine = mine + come.astype(F32)
        return mine

    grad_wout = attn_weight_grad(d_hidden_low, attended, True)
    grad_query = attn_weight_grad(normed_one, d_query, False)
    grad_key = attn_weight_grad(normed_one, d_key, False)
    grad_value = attn_weight_grad(normed_one, d_value, False)

    gains = jnp.stack([gain_one, gain_two])
    gains = sum_all(gains, "dp", [1 << i for i in range((n_dp - 1).bit_length())])
    gains = gather_features(gains)
    return (
        block_output,
        grad_input,
        gains[0],
        gains[1],
        grad_query,
        grad_key,
        grad_value,
        grad_wout,
        grad_gate,
        grad_up,
        grad_down,
    )


def solution(mesh):
    return jax.shard_map(
        per_device,
        mesh=mesh,
        in_specs=(
            P("dp", "tensor"),
            P("dp", "tensor"),
            P(),
            P(),
            P(None, "tensor"),
            P(None, "tensor"),
            P(None, "tensor"),
            P("tensor", None),
            P(None, "tensor"),
            P(None, "tensor"),
            P("tensor", None),
            P(),
        ),
        out_specs=(
            P("dp", "tensor"),
            P("dp", "tensor"),
            P(),
            P(),
            P("dp", "tensor"),
            P("dp", "tensor"),
            P("dp", "tensor"),
            P("tensor", "dp"),
            P("dp", "tensor"),
            P("dp", "tensor"),
            P("tensor", "dp"),
        ),
        check_vma=False,
    )
```

time: 2390 us -> 687 us (0.29)
  waiting for transfers between devices: 1470 us -> 174 us
  blocking collectives: 359 us -> 0 us
  starting transfers between devices: 10.3 us -> 101 us
  other arithmetic: 118 us -> 35.9 us
  matrix products: 285 us -> 233 us
    reduce_scatter x7 -> x0, waiting for transfers between devices: 1030 us -> none  [the longest x1 287 us: per_device(): lax.psum_scatter(grad_down, 'dp', scatter_dimension=1, tiled=True)]
    psum x4 -> x0, waiting for transfers between devices: 331 us -> none  [the longest x1 152 us: per_device(): hidden_state = rows_in + lax.psum(attn_part, 'tensor')]
    all_to_all x2 -> x0, blocking collectives: 230 us -> none  [the longest x1 130 us: per_device(): lax.all_to_all(send_back, 'dp', split_axis=0, concat_axis=0, tiled=True)]
    ppermute x0 -> x79, waiting for transfers between devices: none -> 174 us  [the longest x54 88.4 us: swap(): return lax.ppermute(values, axis, [(i, i ^ mask) for i in range(count)])]
    psum x1 -> x0, blocking collectives: 129 us -> none  [per_device(): gain_one, gain_two = lax.psum((gain_one, gain_two), ('dp', 'tensor'))]
    gather x9 -> x0, local copies, waits for them, and re-layouts: 101 us -> none  [the longest x1 17.3 us: per_device(): grad_output[send_table].reshape(n_groups, PEER, width_part)]
    ppermute x0 -> x79, starting transfers between devices: none -> 101 us  [the longest x54 49.1 us: swap(): return lax.ppermute(values, axis, [(i, i ^ mask) for i in range(count)])]
    all_to_all x2 -> x0, waiting for transfers between devices: 79.1 us -> none  [the longest x1 79.1 us: per_device(): lax.all_to_all(send_input, 'dp', split_axis=0, concat_axis=0, tiled=True)]
  transfers between devices with their start and end apart: 15 -> 79, of which waited for: 10 -> 26; matrix products, arithmetic and copies ran while one was open for 15% -> 52% of each run, Pallas kernels for 0% -> 0%
where the time goes in v1:
time: 687 us; the launch traced here: 680 us
  matrix products  233 us (34%)
  waiting for transfers between devices  174 us (25%)
  local copies, waits for them, and re-layouts  134 us (20%)
  starting transfers between devices  101 us (15%)
  other arithmetic  35.9 us (5%)
    dot_general x44, matrix products, mm(): lax.dot_general(left, right, (((lc,), (rc,)), ((), ())), preferred_elemen...  196 us
    ppermute x54, waiting for transfers between devices, swap(): return lax.ppermute(values, axis, [(i, i ^ mask) for i in range(count)])  88.4 us
    ppermute x54, starting transfers between devices, swap(): return lax.ppermute(values, axis, [(i, i ^ mask) for i in range(count)])  49.1 us
    ppermute x18, waiting for transfers between devices, ring_step(): return lax.ppermute(values, 'dp', pairs)  48.9 us
    ppermute x18, starting transfers between devices, ring_step(): return lax.ppermute(values, 'dp', pairs)  45.5 us
    ppermute x3, waiting for transfers between devices, seat_swap(): return lax.ppermute(values, 'dp', pairs)  36.7 us
    unnamed x193, local copies, waits for them, and re-layouts  31.2 us
    dynamic_update_slice x42, local copies, waits for them, and re-layouts, gather_features(): whole = lax.dynamic_update_slice(whole, block, (0, (me ^ at) * width))  30.9 us
  transfers between devices with their start and end apart: 79, of which 26 were waited for; matrix products, arithmetic and copies ran while one was open for 52% of the time, Pallas kernels for 0%

profile of v1, /device:TPU:0, one launch (start us, length us, event | category | flops | bytes accessed | tf_op | source)
XLA Modules:
  0.0 680.0 jit_solution(12576195811878299156)
XLA Ops:
  13.2 12.3 %copy.71 = bf16[2048,2048]{0,1:T(8,128)(2,1)} copy(bf16[2048,2048]{1,0:T(8,128)(2,1)} %param.22) | data formatting | bytes 16777216 | tf_op args[10]
  26.5 8.5 %constant_dynamic-slice_fusion.18 = (bf16[2048,2,1,512]{0,3,2,1:T(8,128)(2,1)}, bf16[2048,2,1,512]{0,3,2,1:T(8,128)(2,1)}) fusion(bf16[2048,2,2,512]{0,3,2,1:T(8,128)(2,1)} %bitcast.249, s32[]{:T(128)S(6)} %select_n.318, s32[]{:T(128)S(6)} %select_n.317), kind=kLoop, calls=%fused_computation.239 | loop fusion | bytes 16777224 | tf_op jit(solution)/shard_map/jit(dynamic_index_in_dim)/dynamic_slice | solution.py:75
  35.0 9.1 %constant_dynamic-slice_fusion.16 = (bf16[2,1,512,2048]{3,2,1,0:T(8,128)(2,1)}, bf16[2,1,512,2048]{3,2,1,0:T(8,128)(2,1)}, bf16[2,1,512,2048]{3,2,1,0:T(8,128)(2,1)}, bf16[2,1,512,2048]{3,2,1,0:T(8,128)(2,1)}) fusion(bf16[2,2,512,2048]{3,2,1,0:T(8,128)(2,1)} %bitcast.256, s32[]{:T(128)S(6)} %select_n.317, s32[]{:T(128)S(6)} %select_n.318, ...), kind=kLoop, calls=%fused_computation.233 | loop fusion | bytes 33554440 | tf_op jit(solution)/shard_map/jit(dynamic_index_in_dim)/dynamic_slice | solution.py:82
  70.6 3.6 collective-permute-start.68
  81.2 3.8 fusion
  87.1 4.3 fusion.17
  95.7 20.8 %collective-permute-start.72 = (bf16[512,512]{0,1:T(8,128)(2,1)}, bf16[512,512]{0,1:T(8,128)(2,1)S(1)}, u32[]{:S(2)}, u32[]{:S(2)}) collective-permute-start(bf16[512,512]{0,1:T(8,128)(2,1)} %collective-permute-done.68), channel_id=1, source_target_pairs={{0,8},{4,12},{8,16},{12,20},{16,24},{20,28},{24,0},{28,4},{1,9},{5... | collective-permute-start | bytes 1572872 | tf_op jit(solution)/shard_map/ppermute | solution.py:136
  122.7 7.3 %collective-permute-done.72 = bf16[512,512]{0,1:T(8,128)(2,1)S(1)} collective-permute-done((bf16[512,512]{0,1:T(8,128)(2,1)}, bf16[512,512]{0,1:T(8,128)(2,1)S(1)}, u32[]{:S(2)}, u32[]{:S(2)}) %collective-permute-start.72) | collective-permute-done | bytes 524320 | tf_op jit(solution)/shard_map/ppermute | solution.py:136
  135.9 9.0 %collective-permute-done.73 = bf16[512,512]{0,1:T(8,128)(2,1)S(1)} collective-permute-done((bf16[512,512]{0,1:T(8,128)(2,1)S(1)}, bf16[512,512]{0,1:T(8,128)(2,1)S(1)}, u32[]{:S(2)}, u32[]{:S(2)}) %collective-permute-start.73) | collective-permute-done | bytes 524320 | tf_op jit(solution)/shard_map/ppermute | solution.py:30
  145.0 10.1 %collective-permute-done.6 = bf16[512,512]{1,0:T(8,128)(2,1)S(1)} collective-permute-done((bf16[512,512]{1,0:T(8,128)(2,1)S(1)}, bf16[512,512]{1,0:T(8,128)(2,1)S(1)}, u32[]{:S(2)}, u32[]{:S(2)}) %collective-permute-start.6) | collective-permute-done | bytes 524320 | tf_op jit(solution)/shard_map/ppermute | solution.py:30
  162.0 18.4 %fusion.97 = f32[1536,2048]{1,0:T(8,128)} fusion(bf16[2048,2048]{1,0:T(8,128)(2,1)} %param.22, bf16[512,2048]{0,1:T(8,128)(2,1)S(1)} %constant_dynamic-update-slice_fusion, bf16[512,2048]{0,1:T(8,128)(2,1)S(1)} %constant_dynamic-update-slice_fusion.4, bf16[512,2048]{0,1:T(8,128)(2,1)S(1)} %constant_dynamic-update-slice_fusion.8), kind=kOutput, calls=%fused_computation.268 | convolution fusion | flops 12903776256 | bytes 27262976 | tf_op jit(solution)/shard_map/dot_general | solution.py:18
  186.1 10.5 %collective-permute-done.52 = bf16[512,512]{1,0:T(8,128)(2,1)} collective-permute-done((bf16[512,512]{1,0:T(8,128)(2,1)S(1)}, bf16[512,512]{1,0:T(8,128)(2,1)}, u32[]{:S(2)}, u32[]{:S(2)}) %collective-permute-start.52) | collective-permute-done | bytes 524320 | tf_op jit(solution)/shard_map/ppermute | solution.py:136
  196.6 9.7 %collective-permute-start.56 = (bf16[512,512]{1,0:T(8,128)(2,1)}, bf16[512,512]{1,0:T(8,128)(2,1)}, u32[]{:S(2)}, u32[]{:S(2)}) collective-permute-start(bf16[512,512]{1,0:T(8,128)(2,1)} %collective-permute-done.52), channel_id=1, source_target_pairs={{0,8},{4,12},{8,16},{12,20},{16,24},{20,28},{24,0},{28,4},{1,9},{5... | collective-permute-start | bytes 1572872 | tf_op jit(solution)/shard_map/ppermute | solution.py:136
  215.8 10.3 %fusion.105 = f32[512,2048]{1,0:T(8,128)} fusion(bf16[512,2048]{0,1:T(8,128)(2,1)S(1)} %constant_dynamic-update-slice_fusion.36, bf16[2048,2048]{1,0:T(8,128)(2,1)} %param.20), kind=kOutput, calls=%fused_computation.276 | convolution fusion | flops 4294967296 | bytes 14680064 | tf_op jit(solution)/shard_map/dot_general | solution.py:18
  226.1 9.6 %fusion.106 = f32[512,2048]{1,0:T(8,128)} fusion(bf16[512,2048]{0,1:T(8,128)(2,1)S(1)} %constant_dynamic-update-slice_fusion.36, bf16[2048,2048]{1,0:T(8,128)(2,1)} %param.21), kind=kOutput, calls=%fused_computation.277 | convolution fusion | flops 4294967296 | bytes 14680064 | tf_op jit(solution)/shard_map/dot_general | solution.py:18
  235.7 9.4 %multiply_convert_fusion.4 = (bf16[512,2048]{1,0:T(8,128)(2,1)S(1)}, bf16[512,2048]{1,0:T(8,128)(2,1)S(1)}, bf16[512,2048]{1,0:T(8,128)(2,1)S(1)}) fusion(f32[512,2048]{1,0:T(8,128)} %fusion.105, f32[512,2048]{1,0:T(8,128)} %fusion.106, bf16[512,2048]{0,1:T(8,128)(2,1)} %get-tuple-element.70, bf16[2048,2048]{1,0:T(8,128)(2,1)S(1)} %bitcast.267), kind=kOutput, calls=%fused_computation.22 | convolution fusion | flops 4311744512 | bytes 25165824 | tf_op jit(solution)/shard_map/dot_general | solution.py:18
  248.9 3.4 add_convert_fusion.1
  252.3 3.7 fusion.107
  258.2 3.3 convolution_convert_fusion.5
  269.2 3.9 collective-permute-done.60
  293.5 6.3 convert_add_fusion.7
  302.3 3.7 convert_add_fusion.8
  309.5 20.5 %fusion.98 = f32[1536,2048]{1,0:T(8,128)} fusion(bf16[2048,2048]{1,0:T(8,128)(2,1)} %param.20, bf16[512,2048]{0,1:T(8,128)(2,1)} %constant_dynamic-update-slice_fusion.12, bf16[512,2048]{0,1:T(8,128)(2,1)} %constant_dynamic-update-slice_fusion.16, bf16[512,2048]{0,1:T(8,128)(2,1)} %constant_dynamic-update-slice_fusion.20), kind=kOutput, calls=%fused_computation.269 | convolution fusion | flops 12903776256 | bytes 27262976 | tf_op jit(solution)/shard_map/dot_general | solution.py:18
  330.0 6.3 pad_maximum_fusion
  336.3 29.4 %multiply_convert_fusion.1 = (bf16[1536,2048]{1,0:T(8,128)(2,1)}, bf16[1536,2048]{1,0:T(8,128)(2,1)}, bf16[1536,2048]{1,0:T(8,128)(2,1)}) fusion(f32[1536,2048]{1,0:T(8,128)} %fusion.98, f32[1536,2048]{1,0:T(8,128)} %fusion.97, bf16[2048,2048]{1,0:T(8,128)(2,1)} %param.21, bf16[512,2048]{0,1:T(8,128)(2,1)} %constant_dynamic-update-slice_fusion.12, ...), kind=kOutput, calls=%fused_computation.8 | convolution fusion | flops 12954107904 | bytes 58720256 | tf_op jit(solution)/shard_map/dot_general | solution.py:18
  365.7 5.0 fusion.34
  370.7 4.5 fusion.38
  378.4 4.5 fusion.36
  382.9 4.7 fusion.30
  422.2 4.4 convert_add_fusion.1
  426.6 18.0 %collective-permute-done.77 = bf16[256,2048]{1,0:T(8,128)(2,1)} collective-permute-done((bf16[256,2048]{1,0:T(8,128)(2,1)}, bf16[256,2048]{1,0:T(8,128)(2,1)}, u32[]{:S(2)}, u32[]{:S(2)}) %collective-permute-start.77) | collective-permute-done | bytes 1048608 | tf_op jit(solution)/shard_map/ppermute | solution.py:255
  444.7 3.4 convert_add_fusion
  448.1 18.0 %collective-permute-done.78 = bf16[2048,256]{1,0:T(8,128)(2,1)S(1)} collective-permute-done((bf16[2048,256]{1,0:T(8,128)(2,1)}, bf16[2048,256]{1,0:T(8,128)(2,1)S(1)}, u32[]{:S(2)}, u32[]{:S(2)}) %collective-permute-start.78) | collective-permute-done | bytes 1048608 | tf_op jit(solution)/shard_map/ppermute | solution.py:255
  474.4 8.7 %fusion.13 = f32[1024,8,64]{0,2,1:T(8,128)} fusion(bf16[512,8,64]{0,2,1:T(8,128)(2,1)S(1)} %bitcast.311, f32[8,512,1024]{2,1,0:T(8,128)} %copy-done, f32[8,512]{1,0:T(8,128)S(1)} %copy-done.69), kind=kOutput, calls=%fused_computation.54 | convolution fusion | flops 545259520 | bytes 19415040 | tf_op jit(solution)/shard_map/hqk,qhd->khd/dot_general | solution.py:281
  483.1 13.7 %multiply_reduce_fusion = (f32[8,512]{1,0:T(8,128)}, f32[8,512,1024]{2,1,0:T(8,128)}) fusion(f32[8,512,1024]{2,1,0:T(8,128)} %copy-done, f32[8,512]{1,0:T(8,128)} %log_add_fusion, bf16[512,8,64]{0,2,1:T(8,128)(2,1)S(1)} %bitcast.312, bf16[512,8,64]{0,2,1:T(8,128)(2,1)S(1)} %bitcast.329, bf16[512,8,64]{0,2,1:T(8,128)(2,1)} %copy-done.65), kind=kOutput, calls=%fused_computation.1 | convolution fusion | flops 551546880 | bytes 35160064 | tf_op jit(solution)/shard_map/qhd,khd->hqk/dot_general | solution.py:282
  496.9 7.7 %multiply_convert_fusion = bf16[8,512,1024]{2,1,0:T(8,128)(2,1)S(1)} fusion(f32[8,512,1024]{2,1,0:T(8,128)} %get-tuple-element.69, f32[8,512,1024]{2,1,0:T(8,128)S(1)} %bitcast.248, f32[8,512]{1,0:T(8,128)} %get-tuple-element.68, f32[8,512]{1,0:T(8,128)} %log_add_fusion), kind=kLoop, calls=%fused_computation | loop fusion | flops 16777216 | bytes 41975808 | tf_op jit(solution)/shard_map/convert_element_type | solution.py:284
  514.4 6.1 fusion.16
  528.5 11.3 %collective-permute-start.36 = (bf16[1024,512]{1,0:T(8,128)(2,1)}, bf16[1024,512]{1,0:T(8,128)(2,1)}, u32[]{:S(2)}, u32[]{:S(2)}) collective-permute-start(bf16[1024,512]{1,0:T(8,128)(2,1)} %convolution_convert_fusion.3), channel_id=1, source_target_pairs={{0,4},{4,0},{8,12},{12,8},{16,20},{20,16},{24,28},{28,24},{1,5},{5... | collective-permute-start | bytes 3145736 | tf_op jit(solution)/shard_map/ppermute | solution.py:30
  544.8 11.3 %collective-permute-done.48 = bf16[512,1024]{1,0:T(8,128)(2,1)S(1)} collective-permute-done((bf16[512,1024]{1,0:T(8,128)(2,1)S(1)}, bf16[512,1024]{1,0:T(8,128)(2,1)S(1)}, u32[]{:S(2)}, u32[]{:S(2)}) %collective-permute-start.48) | collective-permute-done | bytes 1048608 | tf_op jit(solution)/shard_map/ppermute | solution.py:30
  570.2 3.5 collective-permute-done.49
  581.6 19.4 %collective-permute-done.40 = bf16[1024,512]{1,0:T(8,128)(2,1)S(1)} collective-permute-done((bf16[1024,512]{1,0:T(8,128)(2,1)S(1)}, bf16[1024,512]{1,0:T(8,128)(2,1)S(1)}, u32[]{:S(2)}, u32[]{:S(2)}) %collective-permute-start.40) | collective-permute-done | bytes 1048608 | tf_op jit(solution)/shard_map/ppermute | solution.py:30
  602.7 20.7 %collective-permute-done.44 = bf16[1024,512]{1,0:T(8,128)(2,1)S(1)} collective-permute-done((bf16[1024,512]{1,0:T(8,128)(2,1)S(1)}, bf16[1024,512]{1,0:T(8,128)(2,1)S(1)}, u32[]{:S(2)}, u32[]{:S(2)}) %collective-permute-start.44) | collective-permute-done | bytes 1048608 | tf_op jit(solution)/shard_map/ppermute | solution.py:30
  629.6 5.6 collective-permute-done.45
  635.4 5.5 collective-permute-done.51
  646.6 5.5 collective-permute-done.42
  652.3 5.5 collective-permute-done.46
  658.7 6.0 collective-permute-done.31
  664.7 4.9 collective-permute-start.32
  (505 shorter events, 242.1 us)
Async XLA Ops:
  2.7 47.3 %collective-permute-start.14 = (bf16[512,512]{0,1:T(8,128)(2,1)}, bf16[512,512]{0,1:T(8,128)(2,1)}, u32[]{:S(2)}, u32[]{:S(2)}) collective-permute-start(bf16[512,512]{0,1:T(8,128)(2,1)} %copy.72), channel_id=1, source_target_pairs={{0,2},{1,3},{2,0},{3,1},{4,6},{5,7},{6,4},{7,5},{8,10},{9,11},{10,... | collective-permute-start | bytes 1572872 | tf_op jit(solution)/shard_map/ppermute | solution.py:30
  5.7 50.6 %collective-permute-start.15 = (bf16[512,512]{0,1:T(8,128)(2,1)}, bf16[512,512]{0,1:T(8,128)(2,1)}, u32[]{:S(2)}, u32[]{:S(2)}) collective-permute-start(bf16[512,512]{0,1:T(8,128)(2,1)} %copy.72), channel_id=1, source_target_pairs={{0,1},{1,0},{2,3},{3,2},{4,5},{5,4},{6,7},{7,6},{8,9},{9,8},{10,11... | collective-permute-start | bytes 1572872 | tf_op jit(solution)/shard_map/ppermute | solution.py:30
  7.7 42.4 %collective-permute-start = (bf16[512,512]{0,1:T(8,128)(2,1)}, bf16[512,512]{0,1:T(8,128)(2,1)}, u32[]{:S(2)}, u32[]{:S(2)}) collective-permute-start(bf16[512,512]{0,1:T(8,128)(2,1)} %copy.63), channel_id=1, source_target_pairs={{0,2},{1,3},{2,0},{3,1},{4,6},{5,7},{6,4},{7,5},{8,10},{9,11},{10,... | collective-permute-start | bytes 1572872 | tf_op jit(solution)/shard_map/ppermute | solution.py:30
  7.7 50.4 %collective-permute-start.1 = (bf16[512,512]{0,1:T(8,128)(2,1)}, bf16[512,512]{0,1:T(8,128)(2,1)}, u32[]{:S(2)}, u32[]{:S(2)}) collective-permute-start(bf16[512,512]{0,1:T(8,128)(2,1)} %copy.63), channel_id=1, source_target_pairs={{0,1},{1,0},{2,3},{3,2},{4,5},{5,4},{6,7},{7,6},{8,9},{9,8},{10,11... | collective-permute-start | bytes 1572872 | tf_op jit(solution)/shard_map/ppermute | solution.py:30
  8.2 62.4 %collective-permute-start.64 = (bf16[512,512]{0,1:T(8,128)(2,1)}, bf16[512,512]{0,1:T(8,128)(2,1)}, u32[]{:S(2)}, u32[]{:S(2)}) collective-permute-start(bf16[512,512]{0,1:T(8,128)(2,1)} %copy.72), channel_id=1, source_target_pairs={{0,8},{4,12},{8,16},{12,20},{16,24},{20,28},{24,0},{28,4},{1,9},{5... | collective-permute-start | bytes 1572872 | tf_op jit(solution)/shard_map/ppermute | solution.py:136
  70.6 25.1 %collective-permute-start.68 = (bf16[512,512]{0,1:T(8,128)(2,1)}, bf16[512,512]{0,1:T(8,128)(2,1)}, u32[]{:S(2)}, u32[]{:S(2)}) collective-permute-start(bf16[512,512]{0,1:T(8,128)(2,1)} %collective-permute-done.64), channel_id=1, source_target_pairs={{0,8},{4,12},{8,16},{12,20},{16,24},{20,28},{24,0},{28,4},{1,9},{5... | collective-permute-start | bytes 1572872 | tf_op jit(solution)/shard_map/ppermute | solution.py:136
  74.2 45.2 %collective-permute-start.65 = (bf16[512,512]{0,1:T(8,128)(2,1)}, bf16[512,512]{0,1:T(8,128)(2,1)}, u32[]{:S(2)}, u32[]{:S(2)}) collective-permute-start(bf16[512,512]{0,1:T(8,128)(2,1)} %collective-permute-done.64), channel_id=1, source_target_pairs={{0,2},{1,3},{2,0},{3,1},{4,6},{5,7},{6,4},{7,5},{8,10},{9,11},{10,... | collective-permute-start | bytes 1572872 | tf_op jit(solution)/shard_map/ppermute | solution.py:30
  75.7 44.9 %collective-permute-start.66 = (bf16[512,512]{0,1:T(8,128)(2,1)}, bf16[512,512]{0,1:T(8,128)(2,1)S(1)}, u32[]{:S(2)}, u32[]{:S(2)}) collective-permute-start(bf16[512,512]{0,1:T(8,128)(2,1)} %collective-permute-done.64), channel_id=1, source_target_pairs={{0,1},{1,0},{2,3},{3,2},{4,5},{5,4},{6,7},{7,6},{8,9},{9,8},{10,11... | collective-permute-start | bytes 1572872 | tf_op jit(solution)/shard_map/ppermute | solution.py:30
  93.2 39.4 %collective-permute-start.5 = (bf16[512,1024]{1,0:T(8,128)(2,1)}, bf16[512,1024]{1,0:T(8,128)(2,1)}, u32[]{:S(2)}, u32[]{:S(2)}) collective-permute-start(bf16[512,1024]{1,0:T(8,128)(2,1)} %convolution_convert_fusion.4), channel_id=1, source_target_pairs={{0,1},{1,0},{2,3},{3,2},{4,5},{5,4},{6,7},{7,6},{8,9},{9,8},{10,11... | collective-permute-start | bytes 3145736 | tf_op jit(solution)/shard_map/ppermute | solution.py:30
  95.7 34.4 %collective-permute-start.72 = (bf16[512,512]{0,1:T(8,128)(2,1)}, bf16[512,512]{0,1:T(8,128)(2,1)S(1)}, u32[]{:S(2)}, u32[]{:S(2)}) collective-permute-start(bf16[512,512]{0,1:T(8,128)(2,1)} %collective-permute-done.68), channel_id=1, source_target_pairs={{0,8},{4,12},{8,16},{12,20},{16,24},{20,28},{24,0},{28,4},{1,9},{5... | collective-permute-start | bytes 1572872 | tf_op jit(solution)/shard_map/ppermute | solution.py:136
  132.0 23.5 %collective-permute-start.71 = (bf16[512,512]{0,1:T(8,128)(2,1)S(1)}, bf16[512,512]{0,1:T(8,128)(2,1)S(1)}, u32[]{:S(2)}, u32[]{:S(2)}) collective-permute-start(bf16[512,512]{0,1:T(8,128)(2,1)S(1)} %collective-permute-done.69), channel_id=1, source_target_pairs={{0,1},{1,0},{2,3},{3,2},{4,5},{5,4},{6,7},{7,6},{8,9},{9,8},{10,11... | collective-permute-start | bytes 1572872 | tf_op jit(solution)/shard_map/ppermute | solution.py:30
  134.7 20.4 %collective-permute-start.6 = (bf16[512,512]{1,0:T(8,128)(2,1)S(1)}, bf16[512,512]{1,0:T(8,128)(2,1)S(1)}, u32[]{:S(2)}, u32[]{:S(2)}) collective-permute-start(bf16[512,512]{1,0:T(8,128)(2,1)S(1)} %dynamic-slice_convert_fusion.3), channel_id=1, source_target_pairs={{0,2},{1,3},{2,0},{3,1},{4,6},{5,7},{6,4},{7,5},{8,10},{9,11},{10,... | collective-permute-start | bytes 1572872 | tf_op jit(solution)/shard_map/ppermute | solution.py:30
  160.4 20.8 %collective-permute-start.9 = (bf16[512,512]{1,0:T(8,128)(2,1)S(1)}, bf16[512,512]{1,0:T(8,128)(2,1)}, u32[]{:S(2)}, u32[]{:S(2)}) collective-permute-start(bf16[512,512]{1,0:T(8,128)(2,1)S(1)} %multiply_convert_fusion.7), channel_id=1, source_target_pairs={{0,2},{1,3},{2,0},{3,1},{4,6},{5,7},{6,4},{7,5},{8,10},{9,11},{10,... | collective-permute-start | bytes 1572872 | tf_op jit(solution)/shard_map/ppermute | solution.py:30
  180.4 28.6 %collective-permute-start.10 = (bf16[512,512]{1,0:T(8,128)(2,1)S(1)}, bf16[512,512]{1,0:T(8,128)(2,1)}, u32[]{:S(2)}, u32[]{:S(2)}) collective-permute-start(bf16[512,512]{1,0:T(8,128)(2,1)S(1)} %multiply_convert_fusion.7), channel_id=1, source_target_pairs={{0,1},{1,0},{2,3},{3,2},{4,5},{5,4},{6,7},{7,6},{8,9},{9,8},{10,11... | collective-permute-start | bytes 1572872 | tf_op jit(solution)/shard_map/ppermute | solution.py:30
  180.4 16.2 %collective-permute-start.52 = (bf16[512,512]{1,0:T(8,128)(2,1)S(1)}, bf16[512,512]{1,0:T(8,128)(2,1)}, u32[]{:S(2)}, u32[]{:S(2)}) collective-permute-start(bf16[512,512]{1,0:T(8,128)(2,1)S(1)} %multiply_convert_fusion.7), channel_id=1, source_target_pairs={{0,8},{4,12},{8,16},{12,20},{16,24},{20,28},{24,0},{28,4},{1,9},{5... | collective-permute-start | bytes 1572872 | tf_op jit(solution)/shard_map/ppermute | solution.py:136
  181.2 33.3 %collective-permute-start.11 = (bf16[512,512]{1,0:T(8,128)(2,1)}, bf16[512,512]{1,0:T(8,128)(2,1)}, u32[]{:S(2)}, u32[]{:S(2)}) collective-permute-start(bf16[512,512]{1,0:T(8,128)(2,1)} %collective-permute-done.9), channel_id=1, source_target_pairs={{0,1},{1,0},{2,3},{3,2},{4,5},{5,4},{6,7},{7,6},{8,9},{9,8},{10,11... | collective-permute-start | bytes 1572872 | tf_op jit(solution)/shard_map/ppermute | solution.py:30
  196.6 59.4 %collective-permute-start.56 = (bf16[512,512]{1,0:T(8,128)(2,1)}, bf16[512,512]{1,0:T(8,128)(2,1)}, u32[]{:S(2)}, u32[]{:S(2)}) collective-permute-start(bf16[512,512]{1,0:T(8,128)(2,1)} %collective-permute-done.52), channel_id=1, source_target_pairs={{0,8},{4,12},{8,16},{12,20},{16,24},{20,28},{24,0},{28,4},{1,9},{5... | collective-permute-start | bytes 1572872 | tf_op jit(solution)/shard_map/ppermute | solution.py:136
  208.4 54.3 %collective-permute-start.53 = (bf16[512,512]{1,0:T(8,128)(2,1)}, bf16[512,512]{1,0:T(8,128)(2,1)}, u32[]{:S(2)}, u32[]{:S(2)}) collective-permute-start(bf16[512,512]{1,0:T(8,128)(2,1)} %collective-permute-done.52), channel_id=1, source_target_pairs={{0,2},{1,3},{2,0},{3,1},{4,6},{5,7},{6,4},{7,5},{8,10},{9,11},{10,... | collective-permute-start | bytes 1572872 | tf_op jit(solution)/shard_map/ppermute | solution.py:30
  209.0 57.8 %collective-permute-start.54 = (bf16[512,512]{1,0:T(8,128)(2,1)}, bf16[512,512]{1,0:T(8,128)(2,1)}, u32[]{:S(2)}, u32[]{:S(2)}) collective-permute-start(bf16[512,512]{1,0:T(8,128)(2,1)} %collective-permute-done.52), channel_id=1, source_target_pairs={{0,1},{1,0},{2,3},{3,2},{4,5},{5,4},{6,7},{7,6},{8,9},{9,8},{10,11... | collective-permute-start | bytes 1572872 | tf_op jit(solution)/shard_map/ppermute | solution.py:30
  256.0 17.1 %collective-permute-start.60 = (bf16[512,512]{1,0:T(8,128)(2,1)}, bf16[512,512]{1,0:T(8,128)(2,1)}, u32[]{:S(2)}, u32[]{:S(2)}) collective-permute-start(bf16[512,512]{1,0:T(8,128)(2,1)} %collective-permute-done.56), channel_id=1, source_target_pairs={{0,8},{4,12},{8,16},{12,20},{16,24},{20,28},{24,0},{28,4},{1,9},{5... | collective-permute-start | bytes 1572872 | tf_op jit(solution)/shard_map/ppermute | solution.py:136
  256.4 18.2 %collective-permute-start.57 = (bf16[512,512]{1,0:T(8,128)(2,1)}, bf16[512,512]{1,0:T(8,128)(2,1)}, u32[]{:S(2)}, u32[]{:S(2)}) collective-permute-start(bf16[512,512]{1,0:T(8,128)(2,1)} %collective-permute-done.56), channel_id=1, source_target_pairs={{0,2},{1,3},{2,0},{3,1},{4,6},{5,7},{6,4},{7,5},{8,10},{9,11},{10,... | collective-permute-start | bytes 1572872 | tf_op jit(solution)/shard_map/ppermute | solution.py:30
  258.0 22.3 %collective-permute-start.58 = (bf16[512,512]{1,0:T(8,128)(2,1)}, bf16[512,512]{1,0:T(8,128)(2,1)}, u32[]{:S(2)}, u32[]{:S(2)}) collective-permute-start(bf16[512,512]{1,0:T(8,128)(2,1)} %collective-permute-done.56), channel_id=1, source_target_pairs={{0,1},{1,0},{2,3},{3,2},{4,5},{5,4},{6,7},{7,6},{8,9},{9,8},{10,11... | collective-permute-start | bytes 1572872 | tf_op jit(solution)/shard_map/ppermute | solution.py:30
  262.8 20.1 %collective-permute-start.55 = (bf16[512,512]{1,0:T(8,128)(2,1)}, bf16[512,512]{1,0:T(8,128)(2,1)}, u32[]{:S(2)}, u32[]{:S(2)}) collective-permute-start(bf16[512,512]{1,0:T(8,128)(2,1)} %collective-permute-done.53), channel_id=1, source_target_pairs={{0,1},{1,0},{2,3},{3,2},{4,5},{5,4},{6,7},{7,6},{8,9},{9,8},{10,11... | collective-permute-start | bytes 1572872 | tf_op jit(solution)/shard_map/ppermute | solution.py:30
  266.8 26.7 %collective-permute-start.17 = (bf16[512,1024]{1,0:T(8,128)(2,1)}, bf16[512,1024]{1,0:T(8,128)(2,1)}, u32[]{:S(2)}, u32[]{:S(2)}) collective-permute-start(bf16[512,1024]{1,0:T(8,128)(2,1)} %add_convert_fusion.1), channel_id=1, source_target_pairs={{0,1},{1,0},{2,3},{3,2},{4,5},{5,4},{6,7},{7,6},{8,9},{9,8},{10,11... | collective-permute-start | bytes 3145736 | tf_op jit(solution)/shard_map/ppermute | solution.py:30
  282.9 19.4 %collective-permute-start.12 = (bf16[512,1024]{1,0:T(8,128)(2,1)}, bf16[512,1024]{1,0:T(8,128)(2,1)}, u32[]{:S(2)}, u32[]{:S(2)}) collective-permute-start(bf16[512,1024]{1,0:T(8,128)(2,1)} %convolution_convert_fusion.5), channel_id=1, source_target_pairs={{0,1},{1,0},{2,3},{3,2},{4,5},{5,4},{6,7},{7,6},{8,9},{9,8},{10,11... | collective-permute-start | bytes 3145736 | tf_op jit(solution)/shard_map/ppermute | solution.py:30
  291.4 16.1 %collective-permute-start.63 = (bf16[512,512]{1,0:T(8,128)(2,1)}, bf16[512,512]{1,0:T(8,128)(2,1)}, u32[]{:S(2)}, u32[]{:S(2)}) collective-permute-start(bf16[512,512]{1,0:T(8,128)(2,1)} %collective-permute-done.61), channel_id=1, source_target_pairs={{0,1},{1,0},{2,3},{3,2},{4,5},{5,4},{6,7},{7,6},{8,9},{9,8},{10,11... | collective-permute-start | bytes 1572872 | tf_op jit(solution)/shard_map/ppermute | solution.py:30
  300.7 86.8 %collective-permute-start.18 = (bf16[512,512]{1,0:T(8,128)(2,1)}, bf16[512,512]{1,0:T(8,128)(2,1)S(1)}, u32[]{:S(2)}, u32[]{:S(2)}) collective-permute-start(bf16[512,512]{1,0:T(8,128)(2,1)} %dynamic-slice_convert_fusion.1), channel_id=1, source_target_pairs={{0,2},{1,3},{2,0},{3,1},{4,6},{5,7},{6,4},{7,5},{8,10},{9,11},{10,... | collective-permute-start | bytes 1572872 | tf_op jit(solution)/shard_map/ppermute | solution.py:30
  307.0 89.6 %collective-permute-start.13 = (bf16[512,512]{1,0:T(8,128)(2,1)}, bf16[512,512]{1,0:T(8,128)(2,1)}, u32[]{:S(2)}, u32[]{:S(2)}) collective-permute-start(bf16[512,512]{1,0:T(8,128)(2,1)} %dynamic-slice_convert_fusion.2), channel_id=1, source_target_pairs={{0,2},{1,3},{2,0},{3,1},{4,6},{5,7},{6,4},{7,5},{8,10},{9,11},{10,... | collective-permute-start | bytes 1572872 | tf_op jit(solution)/shard_map/ppermute | solution.py:30
  395.9 26.3 %collective-permute-start.76 = (bf16[256,2048]{1,0:T(8,128)(2,1)}, bf16[256,2048]{1,0:T(8,128)(2,1)}, u32[]{:S(2)}, u32[]{:S(2)}) collective-permute-start(bf16[256,2048]{1,0:T(8,128)(2,1)} %fusion.10), channel_id=1, source_target_pairs={{0,4},{4,0},{8,12},{12,8},{16,20},{20,16},{24,28},{28,24},{1,5},{5... | collective-permute-start | bytes 3145736 | tf_op jit(solution)/shard_map/ppermute | solution.py:255
  402.9 41.7 %collective-permute-start.77 = (bf16[256,2048]{1,0:T(8,128)(2,1)}, bf16[256,2048]{1,0:T(8,128)(2,1)}, u32[]{:S(2)}, u32[]{:S(2)}) collective-permute-start(bf16[256,2048]{1,0:T(8,128)(2,1)} %fusion.11), channel_id=1, source_target_pairs={{0,4},{4,0},{8,12},{12,8},{16,20},{20,16},{24,28},{28,24},{1,5},{5... | collective-permute-start | bytes 3145736 | tf_op jit(solution)/shard_map/ppermute | solution.py:255
  407.5 58.7 %collective-permute-start.78 = (bf16[2048,256]{1,0:T(8,128)(2,1)}, bf16[2048,256]{1,0:T(8,128)(2,1)S(1)}, u32[]{:S(2)}, u32[]{:S(2)}) collective-permute-start(bf16[2048,256]{1,0:T(8,128)(2,1)} %fusion.12), channel_id=1, source_target_pairs={{0,4},{4,0},{8,12},{12,8},{16,20},{20,16},{24,28},{28,24},{1,5},{5... | collective-permute-start | bytes 3145736 | tf_op jit(solution)/shard_map/ppermute | solution.py:255
  415.6 53.7 %collective-permute-start.23 = (bf16[512,512]{1,0:T(8,128)(2,1)}, bf16[512,512]{1,0:T(8,128)(2,1)}, u32[]{:S(2)}, u32[]{:S(2)}) collective-permute-start(bf16[512,512]{1,0:T(8,128)(2,1)} %collective-permute-done.21), channel_id=1, source_target_pairs={{0,1},{1,0},{2,3},{3,2},{4,5},{5,4},{6,7},{7,6},{8,9},{9,8},{10,11... | collective-permute-start | bytes 1572872 | tf_op jit(solution)/shard_map/ppermute | solution.py:30
  512.5 43.6 %collective-permute-start.48 = (bf16[512,1024]{1,0:T(8,128)(2,1)S(1)}, bf16[512,1024]{1,0:T(8,128)(2,1)S(1)}, u32[]{:S(2)}, u32[]{:S(2)}) collective-permute-start(bf16[512,1024]{1,0:T(8,128)(2,1)S(1)} %convolution_convert_fusion), channel_id=1, source_target_pairs={{0,4},{4,0},{8,12},{12,8},{16,20},{20,16},{24,28},{28,24},{1,5},{5... | collective-permute-start | bytes 3145736 | tf_op jit(solution)/shard_map/ppermute | solution.py:30
  526.8 47.1 %collective-permute-start.26 = (bf16[512,1024]{1,0:T(8,128)(2,1)}, bf16[512,1024]{1,0:T(8,128)(2,1)}, u32[]{:S(2)}, u32[]{:S(2)}) collective-permute-start(bf16[512,1024]{1,0:T(8,128)(2,1)} %add_convert_fusion), channel_id=1, source_target_pairs={{0,1},{1,0},{2,3},{3,2},{4,5},{5,4},{6,7},{7,6},{8,9},{9,8},{10,11... | collective-permute-start | bytes 3145736 | tf_op jit(solution)/shard_map/ppermute | solution.py:30
  528.5 50.2 %collective-permute-start.36 = (bf16[1024,512]{1,0:T(8,128)(2,1)}, bf16[1024,512]{1,0:T(8,128)(2,1)}, u32[]{:S(2)}, u32[]{:S(2)}) collective-permute-start(bf16[1024,512]{1,0:T(8,128)(2,1)} %convolution_convert_fusion.3), channel_id=1, source_target_pairs={{0,4},{4,0},{8,12},{12,8},{16,20},{20,16},{24,28},{28,24},{1,5},{5... | collective-permute-start | bytes 3145736 | tf_op jit(solution)/shard_map/ppermute | solution.py:30
  566.8 34.2 %collective-permute-start.40 = (bf16[1024,512]{1,0:T(8,128)(2,1)S(1)}, bf16[1024,512]{1,0:T(8,128)(2,1)S(1)}, u32[]{:S(2)}, u32[]{:S(2)}) collective-permute-start(bf16[1024,512]{1,0:T(8,128)(2,1)S(1)} %copy-done.79), channel_id=1, source_target_pairs={{0,4},{4,0},{8,12},{12,8},{16,20},{20,16},{24,28},{28,24},{1,5},{5... | collective-permute-start | bytes 3145736 | tf_op jit(solution)/shard_map/ppermute | solution.py:30
  568.7 54.7 %collective-permute-start.44 = (bf16[1024,512]{1,0:T(8,128)(2,1)S(1)}, bf16[1024,512]{1,0:T(8,128)(2,1)S(1)}, u32[]{:S(2)}, u32[]{:S(2)}) collective-permute-start(bf16[1024,512]{1,0:T(8,128)(2,1)S(1)} %convolution_convert_fusion.1), channel_id=1, source_target_pairs={{0,4},{4,0},{8,12},{12,8},{16,20},{20,16},{24,28},{28,24},{1,5},{5... | collective-permute-start | bytes 3145736 | tf_op jit(solution)/shard_map/ppermute | solution.py:30
  573.8 50.5 %collective-permute-start.50 = (bf16[512,1,256]{2,0,1:T(8,128)(2,1)S(1)}, bf16[512,1,256]{2,0,1:T(8,128)(2,1)S(1)}, u32[]{:S(2)}, u32[]{:S(2)}) collective-permute-start(bf16[512,1,256]{2,0,1:T(8,128)(2,1)S(1)} %fusion.49), channel_id=1, source_target_pairs={{0,8},{4,12},{8,16},{12,20},{16,24},{20,28},{24,0},{28,4},{1,9},{5... | collective-permute-start | bytes 786440 | tf_op jit(solution)/shard_map/ppermute | solution.py:136
  576.2 65.4 %collective-permute-start.27 = (bf16[512,512]{1,0:T(8,128)(2,1)S(1)}, bf16[512,512]{1,0:T(8,128)(2,1)S(1)}, u32[]{:S(2)}, u32[]{:S(2)}) collective-permute-start(bf16[512,512]{1,0:T(8,128)(2,1)S(1)} %dynamic-slice_convert_fusion), channel_id=1, source_target_pairs={{0,2},{1,3},{2,0},{3,1},{4,6},{5,7},{6,4},{7,5},{8,10},{9,11},{10,... | collective-permute-start | bytes 1572872 | tf_op jit(solution)/shard_map/ppermute | solution.py:30
  580.7 44.6 %collective-permute-start.37 = (bf16[1,256,512]{2,1,0:T(8,128)(2,1)S(1)}, bf16[1,256,512]{2,1,0:T(8,128)(2,1)S(1)}, u32[]{:S(2)}, u32[]{:S(2)}) collective-permute-start(bf16[1,256,512]{2,1,0:T(8,128)(2,1)S(1)} %fusion.59), channel_id=1, source_target_pairs={{0,8},{4,12},{8,16},{12,20},{16,24},{20,28},{24,0},{28,4},{1,9},{5... | collective-permute-start | bytes 786440 | tf_op jit(solution)/shard_map/ppermute | solution.py:136
  601.8 26.3 %collective-permute-start.41 = (bf16[1,256,512]{2,1,0:T(8,128)(2,1)S(1)}, bf16[1,256,512]{2,1,0:T(8,128)(2,1)S(1)}, u32[]{:S(2)}, u32[]{:S(2)}) collective-permute-start(bf16[1,256,512]{2,1,0:T(8,128)(2,1)S(1)} %fusion.60), channel_id=1, source_target_pairs={{0,8},{4,12},{8,16},{12,20},{16,24},{20,28},{24,0},{28,4},{1,9},{5... | collective-permute-start | bytes 786440 | tf_op jit(solution)/shard_map/ppermute | solution.py:136
  624.4 16.5 %collective-permute-start.51 = (bf16[512,1,256]{2,0,1:T(8,128)(2,1)S(1)}, bf16[512,1,256]{2,0,1:T(8,128)(2,1)S(1)}, u32[]{:S(2)}, u32[]{:S(2)}) collective-permute-start(bf16[512,1,256]{2,0,1:T(8,128)(2,1)S(1)} %fusion.48), channel_id=1, source_target_pairs={{0,8},{4,12},{8,16},{12,20},{16,24},{20,28},{24,0},{28,4},{1,9},{5... | collective-permute-start | bytes 786440 | tf_op jit(solution)/shard_map/ppermute | solution.py:136
  625.4 21.1 %collective-permute-start.38 = (bf16[1,256,512]{2,1,0:T(8,128)(2,1)S(1)}, bf16[1,256,512]{2,1,0:T(8,128)(2,1)S(1)}, u32[]{:S(2)}, u32[]{:S(2)}) collective-permute-start(bf16[1,256,512]{2,1,0:T(8,128)(2,1)S(1)} %fusion.58), channel_id=1, source_target_pairs={{0,8},{4,12},{8,16},{12,20},{16,24},{20,28},{24,0},{28,4},{1,9},{5... | collective-permute-start | bytes 786440 | tf_op jit(solution)/shard_map/ppermute | solution.py:136
  628.3 23.8 %collective-permute-start.42 = (bf16[1,256,512]{2,1,0:T(8,128)(2,1)S(1)}, bf16[1,256,512]{2,1,0:T(8,128)(2,1)S(1)}, u32[]{:S(2)}, u32[]{:S(2)}) collective-permute-start(bf16[1,256,512]{2,1,0:T(8,128)(2,1)S(1)} %fusion.55), channel_id=1, source_target_pairs={{0,8},{4,12},{8,16},{12,20},{16,24},{20,28},{24,0},{28,4},{1,9},{5... | collective-permute-start | bytes 786440 | tf_op jit(solution)/shard_map/ppermute | solution.py:136
  635.3 22.5 %collective-permute-start.46 = (bf16[1,256,512]{2,1,0:T(8,128)(2,1)S(1)}, bf16[1,256,512]{2,1,0:T(8,128)(2,1)S(1)}, u32[]{:S(2)}, u32[]{:S(2)}) collective-permute-start(bf16[1,256,512]{2,1,0:T(8,128)(2,1)S(1)} %fusion.52), channel_id=1, source_target_pairs={{0,8},{4,12},{8,16},{12,20},{16,24},{20,28},{24,0},{28,4},{1,9},{5... | collective-permute-start | bytes 786440 | tf_op jit(solution)/shard_map/ppermute | solution.py:136
  646.5 30.6 %collective-permute-start.39 = (bf16[1,256,512]{2,1,0:T(8,128)(2,1)S(1)}, bf16[1,256,512]{2,1,0:T(8,128)(2,1)S(1)}, u32[]{:S(2)}, u32[]{:S(2)}) collective-permute-start(bf16[1,256,512]{2,1,0:T(8,128)(2,1)S(1)} %fusion.57), channel_id=1, source_target_pairs={{0,8},{4,12},{8,16},{12,20},{16,24},{20,28},{24,0},{28,4},{1,9},{5... | collective-permute-start | bytes 786440 | tf_op jit(solution)/shard_map/ppermute | solution.py:136
  652.2 25.8 %collective-permute-start.43 = (bf16[1,256,512]{2,1,0:T(8,128)(2,1)S(1)}, bf16[1,256,512]{2,1,0:T(8,128)(2,1)S(1)}, u32[]{:S(2)}, u32[]{:S(2)}) collective-permute-start(bf16[1,256,512]{2,1,0:T(8,128)(2,1)S(1)} %fusion.54), channel_id=1, source_target_pairs={{0,8},{4,12},{8,16},{12,20},{16,24},{20,28},{24,0},{28,4},{1,9},{5... | collective-permute-start | bytes 786440 | tf_op jit(solution)/shard_map/ppermute | solution.py:136
  657.9 21.0 %collective-permute-start.47 = (bf16[1,256,512]{2,1,0:T(8,128)(2,1)S(1)}, bf16[1,256,512]{2,1,0:T(8,128)(2,1)S(1)}, u32[]{:S(2)}, u32[]{:S(2)}) collective-permute-start(bf16[1,256,512]{2,1,0:T(8,128)(2,1)S(1)} %fusion.51), channel_id=1, source_target_pairs={{0,8},{4,12},{8,16},{12,20},{16,24},{20,28},{24,0},{28,4},{1,9},{5... | collective-permute-start | bytes 786440 | tf_op jit(solution)/shard_map/ppermute | solution.py:136
  (125 other events, 1164.5 us)

commit v2 on v1

v2 whole, which is shorter than its diff:
```python
import functools

import jax
import jax.numpy as jnp
from jax import lax
from jax.experimental import pallas as pl
from jax.experimental.pallas import tpu as pltpu
from jax.sharding import Mesh
from jax.sharding import PartitionSpec as P

HEAD_DIM = 64
PAIR = 2 * HEAD_DIM
ROW_LEN = 2048
MAX_DOC = 512
EPS = 1e-05
THETA = 130000.0
MASKED = -1000000000.0
RING = 4
SCORE_SCALE = HEAD_DIM ** (-0.5)

DP = ("block", "ring", "pair")
TP = ("chip", "core")

F32 = jnp.float32
LOW = jnp.bfloat16


def mm(left, right, lc, rc):
    return lax.dot_general(left, right, (((lc,), (rc,)), ((), ())), preferred_element_type=F32)


def shape_of(dims, kind):
    return jax.ShapeDtypeStruct(dims, kind)


def cost(flops, moved, transcendentals=0):
    return pl.CostEstimate(flops=flops, bytes_accessed=moved, transcendentals=transcendentals)


def whole_spec(dims):
    return pl.BlockSpec(dims, lambda *_: (0,) * len(dims), pipeline_mode=pl.Buffered(1))


def bits_of(size):
    step = size // 2
    while step:
        yield step
        step //= 2


def swap(values, axis, mask):
    count = lax.axis_size(axis)
    return lax.ppermute(values, axis, [(i, i ^ mask) for i in range(count)])


def sum_all(values, axis):
    for at in range((lax.axis_size(axis) - 1).bit_length()):
        values = values + swap(values, axis, 1 << at)
    return values


def gather_blocks(part):
    held = {0: part}
    for mask in bits_of(lax.axis_size(TP)):
        held.update({mask | at: swap(block, TP, mask) for at, block in list(held.items())})
    return [held[at] for at in range(len(held))]


def turn(values, cosine, sine, sign):
    lanes = values.shape[1]
    reps = lanes // PAIR
    if reps > 1:
        cosine = jnp.tile(cosine, (1, reps))
        sine = jnp.tile(sine, (1, reps))
    half = HEAD_DIM // 2
    lane = lax.broadcasted_iota(jnp.int32, values.shape, 1)
    ahead = pltpu.roll(values, lanes - half, 1)
    behind = pltpu.roll(values, half, 1)
    other = jnp.where(lane % HEAD_DIM < half, -ahead, behind)
    return values * cosine + (sign * other) * sine


def split_pairs(rows, owned, odd, keep, send):
    for at in range(rows.shape[1] // (2 * owned)):
        first = rows[:, 2 * at * owned : (2 * at + 1) * owned]
        second = rows[:, (2 * at + 1) * owned : (2 * at + 2) * owned]
        keep[:, at * owned : (at + 1) * owned] = jnp.where(odd, second, first)
        send[:, at * owned : (at + 1) * owned] = jnp.where(odd, first, second)


def norm_rows(blocks, normed, gain, shard):
    width = blocks[0].shape[1]
    total = None
    for block in blocks:
        value = block[...].astype(F32)
        part = jnp.sum(value * value, axis=1, keepdims=True)
        total = part if total is None else total + part
    scale = lax.rsqrt(total / (len(blocks) * width) + EPS)
    for at, block in enumerate(blocks):
        cols = pl.ds(pl.multiple_of((shard ^ at) * width, width), width)
        normed[:, cols] = (block[...].astype(F32) * scale * gain[:, cols]).astype(LOW)
    return scale


def project_in_kernel(count, owned, index, *refs):
    blocks = refs[:count]
    gain, cosine, sine, w_query, w_key, w_value = refs[count : count + 6]
    query, both, keep, send, scale_out, normed = refs[count + 6 :]
    scale = norm_rows(blocks, normed, gain, index[0])
    scale_out[...] = jnp.broadcast_to(scale, scale_out.shape)
    split_pairs(normed, owned, index[1] == 1, keep, send)
    rows = normed[...]
    key = mm(rows, w_key[...], 1, 0)
    both[0] = turn(key, cosine[...], sine[...], 1.0).astype(LOW)
    both[1] = mm(rows, w_value[...], 1, 0).astype(LOW)
    asked = turn(mm(rows, w_query[...], 1, 0), cosine[...], sine[...], 1.0).astype(LOW)
    query[...] = (asked.astype(F32) * SCORE_SCALE).astype(LOW)


def project_in(blocks, gain, cosine, sine, w_query, w_key, w_value, index, owned):
    count = len(blocks)
    tok, width = blocks[0].shape
    wide, local = w_query.shape
    step = min(256, tok)
    row = lambda cols: pl.BlockSpec((step, cols), lambda i, s: (i, 0))
    return pl.pallas_call(
        functools.partial(project_in_kernel, count, owned),
        grid_spec=pltpu.PrefetchScalarGridSpec(
            num_scalar_prefetch=1,
            grid=(tok // step,),
            in_specs=[row(width)] * count
            + [whole_spec((1, wide)), row(PAIR), row(PAIR)]
            + [whole_spec((wide, local))] * 3,
            out_specs=[
                row(local),
                pl.BlockSpec((2, step, local), lambda i, s: (0, i, 0)),
                row(wide // 2),
                row(wide // 2),
                row(128),
            ],
            scratch_shapes=[pltpu.VMEM((step, wide), LOW)],
        ),
        out_shape=[
            shape_of((tok, local), LOW),
            shape_of((2, tok, local), LOW),
            shape_of((tok, wide // 2), LOW),
            shape_of((tok, wide // 2), LOW),
            shape_of((tok, 128), F32),
        ],
        cost_estimate=cost(6 * tok * wide * local, 6 * wide * local + 12 * tok * wide),
        name="project_in",
    )(index, *blocks, gain[None, :], cosine, sine, w_query, w_key, w_value)


def project_halo_kernel(count, index, *refs):
    blocks = refs[:count]
    gain, cosine, sine, w_key, w_value, both, normed = refs[count:]
    norm_rows(blocks, normed, gain, index[0])
    rows = normed[...]
    key = mm(rows, w_key[...], 1, 0)
    both[0] = turn(key, cosine[...], sine[...], 1.0).astype(LOW)
    both[1] = mm(rows, w_value[...], 1, 0).astype(LOW)


def project_halo(blocks, gain, cosine, sine, w_key, w_value, index):
    count = len(blocks)
    tok, width = blocks[0].shape
    wide, local = w_key.shape
    step = min(256, tok)
    row = lambda cols: pl.BlockSpec((step, cols), lambda i, s: (i, 0))
    return pl.pallas_call(
        functools.partial(project_halo_kernel, count),
        grid_spec=pltpu.PrefetchScalarGridSpec(
            num_scalar_prefetch=1,
            grid=(tok // step,),
            in_specs=[row(width)] * count
            + [whole_spec((1, wide)), row(PAIR), row(PAIR)]
            + [whole_spec((wide, local))] * 2,
            out_specs=pl.BlockSpec((2, step, local), lambda i, s: (0, i, 0)),
            scratch_shapes=[pltpu.VMEM((step, wide), LOW)],
        ),
        out_shape=shape_of((2, tok, local), LOW),
        cost_estimate=cost(4 * tok * wide * local, 4 * wide * local + 6 * tok * wide),
        name="project_halo",
    )(index, *blocks, gain[None, :], cosine, sine, w_key, w_value)


def two_heads(values):
    lane = lax.broadcasted_iota(jnp.int32, values.shape, 1)
    zero = jnp.zeros_like(values)
    first = jnp.where(lane < HEAD_DIM, values, zero)
    second = jnp.where(lane < HEAD_DIM, zero, values)
    return jnp.concatenate([first, second], axis=0)


def one_of_two(both):
    rows = both.shape[1] // 2
    at = lax.broadcasted_iota(jnp.int32, (both.shape[0], rows), 0)
    return jnp.where(at < HEAD_DIM, both[:, :rows], both[:, rows:]).T


def window_of(tok, lo, step):
    return tok + lo - MAX_DOC, MAX_DOC + step


def seen(start, tok, lo, step):
    first, size = window_of(tok, lo, step)
    key = lax.broadcasted_iota(jnp.int32, (size, step), 0) + first
    own = lax.broadcasted_iota(jnp.int32, (size, step), 1) + (tok + lo)
    allowed = (key >= start[:, lo : lo + step]) & (key <= own)
    bias = jnp.where(allowed, 0.0, MASKED)
    return jnp.concatenate([bias, bias], axis=1)


def attend_kernel(step, width, order, query, halo, own, start, w_out, *outs):
    attended, log_sum, send, keep, every = outs
    tok = query.shape[0]
    at = pl.program_id(0)
    keys = jnp.concatenate([halo[0], own[0]], axis=0)
    values = jnp.concatenate([halo[1], own[1]], axis=0).T
    for lo in range(0, tok, step):
        first, size = window_of(tok, lo, step)
        asked = two_heads(query[lo : lo + step, :])
        scores = mm(keys[first : first + size], asked, 1, 1) + seen(start, tok, lo, step)
        peak = jnp.max(scores, axis=0, keepdims=True)
        exponent = jnp.exp(scores - peak)
        mass = jnp.sum(exponent, axis=0, keepdims=True)
        prob = (exponent * (1.0 / mass)).astype(LOW)
        found = mm(values[:, first : first + size], prob, 1, 0)
        rows = one_of_two(found).astype(LOW)
        attended[lo : lo + step, :] = rows
        every[lo : lo + step, pl.ds(pl.multiple_of(at * PAIR, PAIR), PAIR)] = rows
        sums = peak + jnp.log(mass)
        log_sum[0, 0:1, lo : lo + step] = sums[:, :step]
        log_sum[0, 1:2, lo : lo + step] = sums[:, step:]

    @pl.when(at == pl.num_programs(0) - 1)
    def _():
        rows = every[...]
        for to in range(2):
            here = slice(to * width, (to + 1) * width)
            away = pl.ds(pl.multiple_of(order[to] * width, width), width)
            send[:, here] = mm(rows, w_out[:, away], 1, 0).astype(LOW)
            home = pl.ds(pl.multiple_of(order[2 + to] * width, width), width)
            keep[:, here] = mm(rows, w_out[:, home], 1, 0)


def attend(query, halo, own, start, w_out, order, width):
    tok, local = query.shape
    pairs = local // PAIR
    step = 128
    both = pl.BlockSpec((2, tok, PAIR), lambda p, s: (0, 0, p))
    wide = pl.BlockSpec((tok, 2 * width), lambda p, s: (0, 0))
    return pl.pallas_call(
        functools.partial(attend_kernel, step, width),
        grid_spec=pltpu.PrefetchScalarGridSpec(
            num_scalar_prefetch=1,
            grid=(pairs,),
            in_specs=[
                pl.BlockSpec((tok, PAIR), lambda p, s: (0, p)),
                both,
                both,
                whole_spec((1, tok)),
                whole_spec(w_out.shape),
            ],
            out_specs=[
                pl.BlockSpec((tok, PAIR), lambda p, s: (0, p)),
                pl.BlockSpec((1, 2, tok), lambda p, s: (p, 0, 0)),
                wide,
                wide,
            ],
            scratch_shapes=[pltpu.VMEM((tok, local), LOW)],
        ),
        out_shape=[
            shape_of((tok, local), LOW),
            shape_of((pairs, 2, tok), F32),
            shape_of((tok, 2 * width), LOW),
            shape_of((tok, 2 * width), F32),
        ],
        cost_estimate=cost(
            8 * tok * (MAX_DOC + step) * local + 8 * tok * local * width,
            12 * tok * local + 20 * tok * width,
            tok * local * 10,
        ),
        name="attend",
    )(order, query, halo, own, start, w_out)


def attend_back_kernel(count, step, owned, index, *refs):
    parts = refs[:count]
    w_out, query, halo, own, start, log_sum, cosine, sine = refs[count : count + 8]
    d_query, d_halo, d_own, row_keep, row_send, d_rows, d_keys, d_values = refs[count + 8 :]
    tok = query.shape[0]

    @pl.when(pl.program_id(0) == 0)
    def _():
        for at, part in enumerate(parts):
            width = part.shape[1]
            d_rows[:, pl.ds(pl.multiple_of((index[0] ^ at) * width, width), width)] = part[...]
        split_pairs(d_rows, owned, index[1] == 1, row_keep, row_send)

    d_attended = mm(d_rows[...], w_out[...], 1, 1).astype(LOW)
    keys = jnp.concatenate([halo[0], own[0]], axis=0)
    values = jnp.concatenate([halo[1], own[1]], axis=0)
    keys_across = keys.T
    d_keys[...] = jnp.zeros_like(d_keys)
    d_values[...] = jnp.zeros_like(d_values)
    for lo in range(0, tok, step):
        first, size = window_of(tok, lo, step)
        here = pl.ds(first, size)
        asked = two_heads(query[lo : lo + step, :])
        grads = two_heads(d_attended[lo : lo + step, :])
        sums = jnp.concatenate(
            [log_sum[0, 0:1, lo : lo + step], log_sum[0, 1:2, lo : lo + step]], axis=1
        )
        scores = mm(keys[first : first + size], asked, 1, 1) + seen(start, tok, lo, step)
        prob = jnp.exp(scores - sums)
        d_prob = mm(values[first : first + size], grads, 1, 1)
        delta = jnp.sum(prob * d_prob, axis=0, keepdims=True)
        d_scores = (prob * (d_prob - delta)).astype(LOW)
        d_values[here, :] += mm(prob.astype(LOW), grads, 1, 0)
        d_keys[here, :] += mm(d_scores, asked, 1, 0)
        found = one_of_two(mm(keys_across[:, first : first + size], d_scores, 1, 0))
        d_query[lo : lo + step, :] = turn(
            found * SCORE_SCALE, cosine[lo : lo + step, :], sine[lo : lo + step, :], -1.0
        ).astype(LOW)
    d_halo[0] = d_keys[:tok].astype(LOW)
    d_halo[1] = d_values[:tok].astype(LOW)
    d_own[0] = d_keys[tok:]
    d_own[1] = d_values[tok:]


def attend_back(parts, w_out, query, halo, own, start, log_sum, cosine, sine, index, owned):
    tok, local = query.shape
    count = len(parts)
    wide = w_out.shape[1]
    pairs = local // PAIR
    step = 128
    both = pl.BlockSpec((2, tok, PAIR), lambda p, s: (0, 0, p))
    return pl.pallas_call(
        functools.partial(attend_back_kernel, count, step, owned),
        grid_spec=pltpu.PrefetchScalarGridSpec(
            num_scalar_prefetch=1,
            grid=(pairs,),
            in_specs=[whole_spec(parts[0].shape)] * count
            + [
                pl.BlockSpec((PAIR, wide), lambda p, s: (p, 0)),
                pl.BlockSpec((tok, PAIR), lambda p, s: (0, p)),
                both,
                both,
                whole_spec((1, tok)),
                pl.BlockSpec((1, 2, tok), lambda p, s: (p, 0, 0)),
                whole_spec((tok, PAIR)),
                whole_spec((tok, PAIR)),
            ],
            out_specs=[
                pl.BlockSpec((tok, PAIR), lambda p, s: (0, p)),
                both,
                both,
                pl.BlockSpec((tok, wide // 2), lambda p, s: (0, 0)),
                pl.BlockSpec((tok, wide // 2), lambda p, s: (0, 0)),
            ],
            scratch_shapes=[
                pltpu.VMEM((tok, wide), LOW),
                pltpu.VMEM((2 * tok, PAIR), F32),
                pltpu.VMEM((2 * tok, PAIR), F32),
            ],
        ),
        out_shape=[
            shape_of((tok, local), LOW),
            shape_of((2, tok, local), LOW),
            shape_of((2, tok, local), F32),
            shape_of((tok, wide // 2), LOW),
            shape_of((tok, wide // 2), LOW),
        ],
        cost_estimate=cost(
            2 * tok * wide * local + 20 * tok * (MAX_DOC + step) * local,
            2 * wide * local + 24 * tok * local,
            tok * local * 10,
        ),
        name="attend_back",
    )(index, *parts, w_out, query, halo, own, start, log_sum, cosine, sine)


def finish_kernel(d_own, back, cosine, sine, out):
    d_key = d_own[0] + back[0].astype(F32)
    out[0] = turn(d_key, cosine[...], sine[...], -1.0).astype(LOW)
    out[1] = (d_own[1] + back[1].astype(F32)).astype(LOW)


def finish_keys(d_own, back, cosine, sine):
    both, tok, local = d_own.shape
    spec = pl.BlockSpec((2, tok, PAIR), lambda p: (0, 0, p))
    return pl.pallas_call(
        finish_kernel,
        grid=(local // PAIR,),
        in_specs=[spec, spec, whole_spec((tok, PAIR)), whole_spec((tok, PAIR))],
        out_specs=spec,
        out_shape=shape_of((2, tok, local), LOW),
        cost_estimate=cost(10 * tok * local, 16 * tok * local),
        name="finish_keys",
    )(d_own, back, cosine, sine)


def partial_kernel(count, added, order, *refs):
    lefts, rights = refs[:count], refs[count : 2 * count]
    rest = refs[2 * count :]
    total = None
    for left, right in zip(lefts, rights):
        part = mm(left[...], right[...], 1, 1)
        total = part if total is None else total + part
    if not added:
        rest[0][...] = total.astype(LOW)
        return
    got, send, keep = rest
    total = total + got[...].astype(F32)
    half = pl.num_programs(0) // 2

    @pl.when(pl.program_id(0) < half)
    def _():
        send[...] = total.astype(LOW)

    @pl.when(pl.program_id(0) >= half)
    def _():
        keep[...] = total


def partial_product(lefts, rights, order, width, got=None):
    tok = lefts[0].shape[-2]
    tile = width // 2
    per = width // tile
    left_specs, right_specs, flops, moved = [], [], 0, 0
    left_args = []
    for left, right in zip(lefts, rights):
        if isinstance(left, tuple):
            array, at = left[0], left[1]
            depth = array.shape[2]
            left_specs.append(
                pl.BlockSpec(
                    (pl.Squeezed(), tok, depth),
                    lambda i, s, at=at: (at, 0, 0),
                    pipeline_mode=pl.Buffered(1),
                )
            )
            left_args.append(array)
        else:
            depth = left.shape[1]
            left_specs.append(whole_spec((tok, depth)))
            left_args.append(left)
        right_specs.append(pl.BlockSpec((tile, depth), lambda i, s: (s[i // per] * per + i % per, 0)))
        flops += 4 * tok * width * depth
        moved += 4 * width * depth + 2 * tok * depth
    block = pl.BlockSpec((tok, tile), lambda i, s: (0, i))
    if got is None:
        extra_in, extra = [], []
        out_specs, out_shape = block, shape_of((tok, 2 * width), LOW)
    else:
        extra_in, extra = [block], [got]
        out_specs = [
            pl.BlockSpec((tok, tile), lambda i, s: (0, jnp.minimum(i, per - 1))),
            pl.BlockSpec((tok, tile), lambda i, s: (0, jnp.maximum(i - per, 0))),
        ]
        out_shape = [shape_of((tok, width), LOW), shape_of((tok, width), F32)]
    return pl.pallas_call(
        functools.partial(partial_kernel, len(lefts), got is not None),
        grid_spec=pltpu.PrefetchScalarGridSpec(
            num_scalar_prefetch=1,
            grid=(2 * per,),
            in_specs=left_specs + right_specs + extra_in,
            out_specs=out_specs,
        ),
        out_shape=out_shape,
        cost_estimate=cost(flops, moved + 6 * tok * width),
        name="partial_product",
    )(order, *left_args, *rights, *extra)


def column_order():
    shard = lax.axis_index(TP)
    core, chip = shard % 2, shard // 2
    order = [2 * (1 - chip) + 1 - core, 2 * chip + 1 - core, 2 * (1 - chip) + core, shard]
    return jnp.stack(order).astype(jnp.int32)


def finish_reduce(send, keep):
    total = keep + swap(send, TP, 1).astype(F32)
    width = total.shape[1] // 2
    return total[:, width:], swap(total[:, :width].astype(LOW), TP, 2)


def assemble(parts, whole, shard):
    if len(parts[0].shape) == 2:
        for at, part in enumerate(parts):
            width = part.shape[1]
            whole[:, pl.ds(pl.multiple_of((shard ^ at) * width, width), width)] = part[...]
        return
    for at, part in enumerate(parts):
        _, chips, cores, rows, width = part.shape
        for place in range(chips * cores):
            whole[at * rows : (at + 1) * rows, place * width : (place + 1) * width] = part[
                0, place // cores, place % cores
            ]


def part_specs(parts, places):
    if places is None:
        rows, width = parts[0].shape
        return [whole_spec(part.shape) for part in parts], rows, len(parts) * width
    _, chips, cores, rows, width = parts[0].shape
    specs = [
        pl.BlockSpec(
            (1, chips, cores, rows, width),
            lambda h, s, place=place: (s[2 + place], 0, 0, 0, 0),
            pipeline_mode=pl.Buffered(1),
        )
        for place in places
    ]
    return specs, rows * len(places), chips * cores * width


def pick_owned(whole, owned, place, segments):
    size = owned.shape[1] // segments
    every = whole.shape[1] // segments
    for at in range(segments):
        first = pl.multiple_of(at * every + place * size, size)
        owned[:, at * size : (at + 1) * size] = whole[:, pl.ds(first, size)]


def back_units_kernel(count, segments, index, *refs):
    parts = refs[:count]
    w_down, d_inner, owned, whole = refs[count:]

    @pl.when(pl.program_id(0) == 0)
    def _():
        assemble(parts, whole, index[0])
        pick_owned(whole, owned, index[1], segments)

    d_inner[...] = mm(whole[...], w_down[...], 1, 1).astype(LOW)


def back_units(parts, places, w_down, index, ring, segments):
    specs, rows, wide = part_specs(parts, places)
    count = len(specs)
    parts = parts * (count // len(parts))
    units = w_down.shape[0]
    tile = min(512, units)
    return pl.pallas_call(
        functools.partial(back_units_kernel, count, segments),
        grid_spec=pltpu.PrefetchScalarGridSpec(
            num_scalar_prefetch=1,
            grid=(units // tile,),
            in_specs=specs + [pl.BlockSpec((tile, wide), lambda h, s: (h, 0))],
            out_specs=[
                pl.BlockSpec((rows, tile), lambda h, s: (0, h)),
                pl.BlockSpec((rows, wide // ring), lambda h, s: (0, 0)),
            ],
            scratch_shapes=[pltpu.VMEM((rows, wide), LOW)],
        ),
        out_shape=[shape_of((rows, units), LOW), shape_of((rows, wide // ring), LOW)],
        cost_estimate=cost(2 * rows * wide * units, 2 * wide * units + 2 * rows * (wide + units)),
        name="back_units",
    )(index, *parts, w_down)


def units_of(rows, w_gate, w_up, d_inner):
    gate = mm(rows, w_gate, 1, 0)
    up = mm(rows, w_up, 1, 0)
    sig = jax.nn.sigmoid(gate)
    held = gate * sig
    d_inner = d_inner.astype(F32)
    inner = (held * up).astype(LOW)
    d_gate = (d_inner * up * sig * (1.0 + gate * (1.0 - sig))).astype(LOW)
    return inner, d_gate, (d_inner * held).astype(LOW)


def far_units_kernel(count, segments, index, *refs):
    parts = refs[:count]
    d_inner, w_gate, w_up, inner, d_gate, d_up, owned, whole = refs[count:]

    @pl.when(pl.program_id(0) == 0)
    def _():
        assemble(parts, whole, index[0])
        pick_owned(whole, owned, index[1], segments)

    inner[...], d_gate[...], d_up[...] = units_of(
        whole[...], w_gate[...], w_up[...], d_inner[...]
    )


def far_units(parts, places, d_inner, w_gate, w_up, index, ring, segments):
    specs, rows, wide = part_specs(parts, places)
    count = len(specs)
    parts = parts * (count // len(parts))
    units = w_gate.shape[1]
    tile = min(512, units)
    unit = pl.BlockSpec((rows, tile), lambda h, s: (0, h))
    weight = pl.BlockSpec((wide, tile), lambda h, s: (0, h))
    return pl.pallas_call(
        functools.partial(far_units_kernel, count, segments),
        grid_spec=pltpu.PrefetchScalarGridSpec(
            num_scalar_prefetch=1,
            grid=(units // tile,),
            in_specs=specs + [unit, weight, weight],
            out_specs=[unit] * 3 + [pl.BlockSpec((rows, wide // ring), lambda h, s: (0, 0))],
            scratch_shapes=[pltpu.VMEM((rows, wide), LOW)],
        ),
        out_shape=[shape_of((rows, units), LOW)] * 3 + [shape_of((rows, wide // ring), LOW)],
        cost_estimate=cost(
            4 * rows * wide * units, 4 * wide * units + 8 * rows * units, rows * units
        ),
        name="far_units",
    )(index, *parts, d_inner, w_gate, w_up)


def own_units_kernel(count, segments, index, order, *refs):
    parts, grad_parts = refs[:count], refs[count : count + 1]
    w_gate, w_up, w_down, inner, d_gate, d_up, owned, grad_owned = refs[count + 1 : count + 9]
    back_send, back_keep, out_send, out_keep, whole, grads, back_sum, out_sum = refs[count + 9 :]
    step = pl.program_id(0)
    wide = whole.shape[1]
    width = parts[0].shape[1]

    @pl.when(step == 0)
    def _():
        assemble(parts, whole, index[0])
        pick_owned(whole, owned, index[1], segments)
        assemble(grad_parts, grads, index[0])
        pick_owned(grads, grad_owned, index[1], segments)
        back_sum[...] = jnp.zeros_like(back_sum)
        out_sum[...] = jnp.zeros_like(out_sum)

    d_inner = mm(grads[...], w_down[...], 1, 1)
    units = units_of(whole[...], w_gate[...], w_up[...], d_inner)
    inner[...], d_gate[...], d_up[...] = units
    for lo in range(0, wide, width):
        here = slice(lo, lo + width)
        back_sum[:, here] += mm(units[1], w_gate[here, :], 1, 1) + mm(units[2], w_up[here, :], 1, 1)
        out_sum[:, here] += mm(units[0], w_down[:, here], 1, 0)

    @pl.when(step == pl.num_programs(0) - 1)
    def _():
        for to in range(2):
            here = slice(to * width, (to + 1) * width)
            away = pl.ds(pl.multiple_of(order[to] * width, width), width)
            home = pl.ds(pl.multiple_of(order[2 + to] * width, width), width)
            back_send[:, here] = back_sum[:, away].astype(LOW)
            back_keep[:, here] = back_sum[:, home]
            out_send[:, here] = out_sum[:, away].astype(LOW)
            out_keep[:, here] = out_sum[:, home]


def own_units(parts, grad_every, w_gate, w_up, w_down, index, order, ring, segments):
    count = len(parts)
    rows, width = parts[0].shape
    wide, units = w_gate.shape
    tile = min(256, units)
    unit = pl.BlockSpec((rows, tile), lambda h, s, o: (0, h))
    weight = pl.BlockSpec((wide, tile), lambda h, s, o: (0, h))
    half = pl.BlockSpec((rows, 2 * width), lambda h, s, o: (0, 0))
    mine = pl.BlockSpec((rows, wide // ring), lambda h, s, o: (0, 0))
    grads = pl.BlockSpec(
        (1,) + grad_every.shape[1:],
        lambda h, s, o: (s[1], 0, 0, 0, 0),
        pipeline_mode=pl.Buffered(1),
    )
    return pl.pallas_call(
        functools.partial(own_units_kernel, count, segments),
        grid_spec=pltpu.PrefetchScalarGridSpec(
            num_scalar_prefetch=2,
            grid=(units // tile,),
            in_specs=[whole_spec((rows, width))] * count
            + [grads, weight, weight, pl.BlockSpec((tile, wide), lambda h, s, o: (h, 0))],
            out_specs=[unit] * 3 + [mine] * 2 + [half] * 4,
            scratch_shapes=[
                pltpu.VMEM((rows, wide), LOW),
                pltpu.VMEM((rows, wide), LOW),
                pltpu.VMEM((rows, wide), F32),
                pltpu.VMEM((rows, wide), F32),
            ],
        ),
        out_shape=[shape_of((rows, units), LOW)] * 3
        + [shape_of((rows, wide // ring), LOW)] * 2
        + [shape_of((rows, 2 * width), LOW), shape_of((rows, 2 * width), F32)] * 2,
        cost_estimate=cost(
            12 * rows * wide * units, 6 * wide * units + 8 * rows * units, rows * units
        ),
        name="own_units",
    )(index, order, *parts, grad_every, w_gate, w_up, w_down)


def ffn_grads_kernel(owned, counts, seat, *refs):
    groups, at = [], 0
    for count in counts:
        groups.append(refs[at : at + count])
        at += count
    normed, grads, d_gate, d_up, inner = groups
    send, keep, normed_across, grads_across = refs[at:]

    @pl.when(pl.program_id(0) == 0)
    def _():
        other = seat[0] == 1
        for parts, across in ((normed, normed_across), (grads, grads_across)):
            lo = 0
            for part in parts:
                rows = part.shape[0]
                whole = part[...]
                first, second = whole[:, :owned].T, whole[:, owned:].T
                across[:owned, lo : lo + rows] = jnp.where(other, first, second)
                across[owned:, lo : lo + rows] = jnp.where(other, second, first)
                lo += rows

    for to, (across, parts) in enumerate(
        ((normed_across, d_gate), (normed_across, d_up), (grads_across, inner))
    ):
        total, lo = None, 0
        for part in parts:
            rows = part.shape[0]
            term = mm(across[:, lo : lo + rows], part[...], 1, 0)
            total = term if total is None else total + term
            lo += rows
        send[to] = total[:owned].astype(LOW)
        keep[to] = total[owned:]


def ffn_grads(normed, grads, d_gate, d_up, inner, seat, owned):
    groups = [normed, grads, d_gate, d_up, inner]
    counts = [len(group) for group in groups]
    rows = sum(part.shape[0] for part in normed)
    units = inner[0].shape[1]
    tile = min(512, units)
    specs = []
    for group in groups[:2]:
        specs += [whole_spec((part.shape[0], 2 * owned)) for part in group]
    for group in groups[2:]:
        specs += [pl.BlockSpec((part.shape[0], tile), lambda h, s: (0, h)) for part in group]
    stack = pl.BlockSpec((3, owned, tile), lambda h, s: (0, 0, h))
    return pl.pallas_call(
        functools.partial(ffn_grads_kernel, owned, counts),
        grid_spec=pltpu.PrefetchScalarGridSpec(
            num_scalar_prefetch=1,
            grid=(units // tile,),
            in_specs=specs,
            out_specs=[stack, stack],
            scratch_shapes=[pltpu.VMEM((2 * owned, rows), LOW)] * 2,
        ),
        out_shape=[shape_of((3, owned, units), LOW), shape_of((3, owned, units), F32)],
        cost_estimate=cost(12 * rows * owned * units, 6 * rows * units + 18 * owned * units),
        name="ffn_grads",
    )(seat[None].astype(jnp.int32), *[part for group in groups for part in group])


def add_grads_kernel(keep, got, gate, up, down):
    gate[...] = keep[0] + got[0].astype(F32)
    up[...] = keep[1] + got[1].astype(F32)
    down[...] = (keep[2] + got[2].astype(F32)).T


def add_grads(keep, got):
    _, owned, units = keep.shape
    tile = min(512, units)
    stack = pl.BlockSpec((3, owned, tile), lambda h: (0, 0, h))
    wide = pl.BlockSpec((owned, tile), lambda h: (0, h))
    return pl.pallas_call(
        add_grads_kernel,
        grid=(units // tile,),
        in_specs=[stack, stack],
        out_specs=[wide, wide, pl.BlockSpec((tile, owned), lambda h: (h, 0))],
        out_shape=[shape_of((owned, units), F32)] * 2 + [shape_of((units, owned), F32)],
        cost_estimate=cost(3 * owned * units, 30 * owned * units),
        name="add_grads",
    )(keep, got)


def per_device(
    block_input,
    grad_output,
    norm_attn,
    norm_ffn,
    w_query,
    w_key,
    w_value,
    w_out,
    w_gate,
    w_up,
    w_down,
    doc_lengths,
):
    tok, width = block_input.shape
    width_all = norm_attn.shape[0]
    n_dp = lax.axis_size(DP)
    me = lax.axis_index(DP)
    shard = lax.axis_index(TP)
    ring = min(RING, n_dp // 2)
    blocks = n_dp // (2 * ring)
    pair_at = me % 2
    ring_at = (me // 2) % ring
    block_at = me // (2 * ring)
    owned = width_all // n_dp
    seat = block_at * 2 + pair_at
    seats = blocks * 2
    index = jnp.stack([shard, pair_at]).astype(jnp.int32)
    ring_index = jnp.stack(
        [shard, ring_at] + [(ring_at + step) % ring for step in range(1, ring)]
    ).astype(jnp.int32)

    def seat_swap(values, mask):
        pairs = []
        for i in range(n_dp):
            b, k, c = i // (2 * ring), (i // 2) % ring, i % 2
            s = (b * 2 + c) ^ mask
            pairs.append((i, ((s // 2) * ring + k) * 2 + s % 2))
        return lax.ppermute(values, DP, pairs)

    row_groups = ROW_LEN // tok
    halo_pairs = [(i, i + 1) for i in range(n_dp) if 0 < i % row_groups < row_groups - 1]
    back_pairs = [(j, i) for i, j in halo_pairs]

    starts = jnp.cumsum(doc_lengths, dtype=jnp.int32) - doc_lengths
    token_ids = (me - 1) * tok + jnp.arange(2 * tok, dtype=jnp.int32)
    doc_start = jnp.max(
        jnp.where(starts[:, None] <= token_ids[None, :], starts[:, None], 0), axis=0
    )
    position = (token_ids - doc_start).astype(F32)
    start = (doc_start[tok:] - (me - 1) * tok)[None, :]
    lane = jnp.arange(PAIR, dtype=jnp.int32) % (HEAD_DIM // 2)
    frequency = THETA ** (-lane.astype(F32) * 2.0 / HEAD_DIM)
    angles = position[:, None] * frequency[None, :]
    cosine, sine = jnp.cos(angles[tok:]), jnp.sin(angles[tok:])
    halo_cosine, halo_sine = jnp.cos(angles[:tok]), jnp.sin(angles[:tok])

    my_gain_one = lax.dynamic_slice_in_dim(norm_attn, shard * width, width)
    my_gain_two = lax.dynamic_slice_in_dim(norm_ffn, shard * width, width)
    my_rows = block_input.astype(F32)
    my_grad = grad_output.astype(F32)

    order = column_order()
    away, home = order[:2], order[2:]

    def ring_send(values, shift):
        pairs = []
        for i in range(n_dp):
            b, k, c = i // (2 * ring), (i // 2) % ring, i % 2
            pairs.append((i, (b * ring + (k + shift) % ring) * 2 + c))
        return lax.ppermute(values, DP, pairs)

    def after(values, *others):
        return lax.optimization_barrier((values, *others))[0]

    row_parts = gather_blocks(block_input)
    halo_rows = lax.ppermute(block_input, DP, halo_pairs)
    halo_parts = gather_blocks(halo_rows)
    grad_every = lax.all_gather(after(grad_output, halo_rows, row_parts[-2]), ("ring",) + TP, axis=0)
    grad_every = grad_every.reshape(ring, lax.axis_size("chip"), 2, tok, width)

    query, own, normed_keep, normed_send, scale_wide = project_in(
        row_parts, norm_attn, cosine, sine, w_query, w_key, w_value, index, owned
    )
    scale_one = scale_wide[:, :1]
    normed_far = swap(normed_send, "pair", 1)
    halo = project_halo(
        halo_parts, norm_attn, halo_cosine, halo_sine, w_key, w_value, index
    )
    attended, log_sum, send, keep = attend(query, halo, own, start, w_out, order, width)
    send = after(send, normed_far)

    mine, come = finish_reduce(send, keep)
    hidden = my_rows + (mine + come.astype(F32))
    square = sum_all(jnp.sum(hidden * hidden, axis=1), TP)
    scale_two = lax.rsqrt(square / width_all + EPS)[:, None]
    normed_slice = (hidden * scale_two * my_gain_two).astype(LOW)
    normed_parts = gather_blocks(normed_slice)
    normed_every = lax.all_gather(normed_slice, ("ring",) + TP, axis=0)
    normed_every = normed_every.reshape(ring, lax.axis_size("chip"), 2, tok, width)

    found = own_units(
        normed_parts, grad_every, w_gate, w_up, w_down, ring_index, order, ring, blocks
    )
    pieces, units_grad = [found[:4]], [found[4]]
    send, keep, out_send, out_keep = found[5:]
    groups = [range(ring - 1)] if ring < 3 else [range(1), range(1, ring - 1)]

    def more_units(at, *waits):
        grads, rows = after(grad_every, *waits), after(normed_every, *waits)
        d_inner, grad_owned = back_units([grads], groups[at], w_down, ring_index, ring, blocks)
        found = far_units(
            [rows], groups[at], d_inner, w_gate, w_up, ring_index, ring, blocks
        )
        pieces.append(found)
        units_grad.append(grad_owned)
        return d_inner, found[0]

    first_back, first_units = more_units(0, send)

    mine, come = finish_reduce(send, keep)
    come = after(come, first_back)
    d_normed_two = mine + come.astype(F32)
    gain_two = jnp.sum(d_normed_two * hidden * scale_two, axis=0)
    weighted = d_normed_two * my_gain_two
    mean_two = sum_all(jnp.sum(weighted * hidden, axis=1), TP) / width_all
    d_hidden = my_grad + scale_two * (
        weighted - hidden * scale_two * scale_two * mean_two[:, None]
    )
    d_hidden_parts = after(gather_blocks(d_hidden.astype(LOW)), first_units)

    d_query, d_halo, d_own, hidden_keep, hidden_send = attend_back(
        d_hidden_parts, w_out, query, halo, own, start, log_sum, cosine, sine, index, owned
    )
    back = lax.ppermute(d_halo, DP, back_pairs)
    out_come = swap(mm(attended, hidden_send, 0, 0).astype(LOW), "pair", 1)
    far_query = swap(d_query, "pair", 1)
    if len(groups) > 1:
        back = after(back, more_units(1, d_query)[1])
    d_both = finish_keys(d_own, back, cosine, sine)
    far_both = swap(d_both, "pair", 1)
    units, units_gate, units_up, units_normed = (list(part) for part in zip(*pieces))

    if owned % 128 == 0 and seats == 2:
        units_gate[-1] = after(units_gate[-1], d_both)
        far_send, near_keep = ffn_grads(
            units_normed, units_grad, units_gate, units_up, units, seat, owned
        )
        d_both, out_come, far_query = after((d_both, out_come, far_query), far_send)
        grad_gate, grad_up, grad_down = add_grads(near_keep, seat_swap(far_send, 1))
    else:

        def seat_grads(at):
            def columns(rows):
                return lax.dynamic_slice_in_dim(rows, at * owned, owned, 1)

            def product(rows, hidden_units):
                return mm(columns(jnp.concatenate(rows)), jnp.concatenate(hidden_units), 0, 0)

            return jnp.stack(
                [
                    product(units_normed, units_gate),
                    product(units_normed, units_up),
                    product(units_grad, units),
                ]
            )

        total = seat_grads(seat)
        for mask in range(1, seats):
            total = total + seat_swap(seat_grads(seat ^ mask).astype(LOW), mask).astype(F32)
        grad_gate, grad_up, grad_down = total[0], total[1], total[2].T

    lefts = [d_query, (d_both, 0), (d_both, 1)]
    rights = [w_query, w_key, w_value]
    sent = partial_product(lefts, rights, away, width)
    send, mine = partial_product(lefts, rights, home, width, swap(sent, TP, 1))
    d_normed_one = mine + swap(send, TP, 2).astype(F32)
    gain_one = jnp.sum(d_normed_one * my_rows * scale_one, axis=0)
    weighted = d_normed_one * my_gain_one
    mean_one = sum_all(jnp.sum(weighted * my_rows, axis=1), TP) / width_all
    d_rows = d_hidden + scale_one * (
        weighted - my_rows * scale_one * scale_one * mean_one[:, None]
    )
    grad_input = d_rows.astype(LOW)

    mine, come = finish_reduce(out_send, out_keep)
    block_output = (hidden + (mine + come.astype(F32))).astype(LOW)

    def around(total, axis):
        mine = lax.dynamic_index_in_dim(total, ring_at, axis, False)
        for shift in range(1, ring):
            other = lax.dynamic_index_in_dim(total, (ring_at + shift) % ring, axis, False)
            mine = mine + ring_send(other.astype(LOW), shift).astype(F32)
        total = mine
        mine = lax.dynamic_index_in_dim(total, block_at, axis - 1, False)
        for mask in range(1, blocks):
            other = lax.dynamic_index_in_dim(total, block_at ^ mask, axis - 1, False)
            mine = mine + swap(other.astype(LOW), DP, mask * 2 * ring).astype(F32)
        return mine

    total = mm(attended, hidden_keep, 0, 0) + out_come.astype(F32)
    grad_wout = around(total.reshape(-1, blocks, ring, owned), 2)

    def in_grad(near, far):
        total = mm(normed_keep, near, 0, 0) + mm(normed_far, far, 0, 0)
        return total.reshape(blocks, ring, owned, -1)

    grad_query = around(in_grad(d_query, far_query), 1)
    pair_grads = around(
        jnp.concatenate(
            [in_grad(d_both[0], far_both[0]), in_grad(d_both[1], far_both[1])], axis=3
        ),
        1,
    )
    local = d_query.shape[1]
    grad_key, grad_value = pair_grads[:, :local], pair_grads[:, local:]

    gains = sum_all(jnp.stack([gain_one, gain_two]), DP)
    gain_parts = gather_blocks(gains)
    gains = jnp.zeros((2, width_all), F32)
    for at, part in enumerate(gain_parts):
        gains = lax.dynamic_update_slice(gains, part, (0, (shard ^ at) * width))
    return (
        block_output,
        grad_input,
        gains[0],
        gains[1],
        grad_query,
        grad_key,
        grad_value,
        grad_wout,
        grad_gate,
        grad_up,
        grad_down,
    )


def solution(mesh):
    n_dp, n_tp = mesh.shape["dp"], mesh.shape["tensor"]
    ring = min(RING, n_dp // 2)
    parts = mesh.devices.reshape(n_dp // (2 * ring), ring, 2, n_tp // 2, 2)
    finer = Mesh(parts, DP + TP)
    rows, cols = P(DP, TP), P(TP, DP)
    wide, tall = P(None, TP), P(TP, None)
    return jax.shard_map(
        per_device,
        mesh=finer,
        in_specs=(rows, rows, P(), P(), wide, wide, wide, tall, wide, wide, tall, P()),
        out_specs=(rows, rows, P(), P(), rows, rows, rows, cols, rows, rows, cols),
        check_vma=False,
    )
```

time: 687 us -> 476 us (0.69)
  matrix products: 233 us -> 10.3 us
  Pallas kernels: 0 us -> 222 us
  local copies, waits for them, and re-layouts: 134 us -> 21.2 us
  waiting for transfers between devices: 174 us -> 117 us
  starting transfers between devices: 101 us -> 65.1 us
  other arithmetic: 35.9 us -> 20.7 us
  between operations: 2.81 us -> 14.9 us
    pallas_call x0 -> x14, Pallas kernels: none -> 222 us  [the longest x1 43.9 us: own_units(): pl.pallas_call(functools.partial(own_units_kernel, count, segments), grid...]
    dot_general x44 -> x8, matrix products: 196 us -> 10.3 us  [mm(): lax.dot_general(left, right, (((lc,), (rc,)), ((), ())), preferred_elemen...]
    ppermute x25 -> x12, waiting for transfers between devices: 85.6 us -> 36.8 us  [the longest x9 36.7 us: ring_send(): return lax.ppermute(values, DP, pairs)]
    dot_general x6 -> x0, matrix products: 37.4 us -> none  [the longest x1 13.7 us: per_device(): jnp.einsum('qhd,khd->hqk', d_attended, values, preferred_element_type=F32)]
    dynamic_update_slice x42 -> x3, local copies, waits for them, and re-layouts: 30.9 us -> 0.03 us  [per_device(): gains = lax.dynamic_update_slice(gains, part, (0, (shard ^ at) * width))]
    ppermute x18 -> x0, local copies, waits for them, and re-layouts: 25.9 us -> none  [the longest x15 21.3 us: swap(): return lax.ppermute(values, axis, [(i, i ^ mask) for i in range(count)])]
    unnamed x193 -> x73, local copies, waits for them, and re-layouts: 31.2 us -> 6.04 us
    dynamic_slice x9 -> x2, local copies, waits for them, and re-layouts: 29.1 us -> 4.23 us  [the longest x1 2.8 us: around(): mine = lax.dynamic_index_in_dim(total, ring_at, axis, False)]
  transfers between devices with their start and end apart: 79 -> 50, of which waited for: 26 -> 22; matrix products, arithmetic and copies ran while one was open for 52% -> 10% of each run, Pallas kernels for 0% -> 41%
where the time goes in v2:
time: 476 us; the launch traced here: 471 us
  Pallas kernels  222 us (47%)
  waiting for transfers between devices  117 us (25%)
  starting transfers between devices  65.1 us (14%)
  local copies, waits for them, and re-layouts  21.2 us (4%)
  other arithmetic  20.7 us (4%)
  between operations  14.9 us (3%)
  matrix products  10.3 us (2%)
    ppermute x36, waiting for transfers between devices, swap(): return lax.ppermute(values, axis, [(i, i ^ mask) for i in range(count)])  80.4 us
    pallas_call x1, Pallas kernels, own_units(): pl.pallas_call(functools.partial(own_units_kernel, count, segments), grid...  43.9 us
    pallas_call x2, Pallas kernels, far_units(): pl.pallas_call(functools.partial(far_units_kernel, count, segments), grid...  43.6 us
    ppermute x9, waiting for transfers between devices, ring_send(): return lax.ppermute(values, DP, pairs)  36.7 us
    ppermute x9, starting transfers between devices, ring_send(): return lax.ppermute(values, DP, pairs)  35.3 us
    pallas_call x2, Pallas kernels, back_units(): pl.pallas_call(functools.partial(back_units_kernel, count, segments), gri...  32.4 us
    ppermute x36, starting transfers between devices, swap(): return lax.ppermute(values, axis, [(i, i ^ mask) for i in range(count)])  26.7 us
    pallas_call x1, Pallas kernels, ffn_grads(): pl.pallas_call(functools.partial(ffn_grads_kernel, owned, counts), grid_s...  21.6 us
  transfers between devices with their start and end apart: 50, of which 22 were waited for; matrix products, arithmetic and copies ran while one was open for 10% of the time, Pallas kernels for 41%

profile of v2, /device:TPU:0, one launch (start us, length us, event | category | flops | bytes accessed | tf_op | source)
XLA Modules:
  0.0 471.2 jit_solution(8730881414401172662)
XLA Ops:
  7.2 3.0 collective-permute-start.1
  10.9 11.4 %collective-permute-done.1.refs_2_ = bf16[512,512]{1,0:T(8,128)(2,1)S(1)} collective-permute-done((bf16[512,512]{1,0:T(8,128)(2,1)}, bf16[512,512]{1,0:T(8,128)(2,1)S(1)}, u32[]{:S(2)}, u32[]{:S(2)}) %collective-permute-start.1) | collective-permute-done | bytes 524320 | tf_op jit(solution)/shard_map/ppermute | solution.py:53
  24.9 1.8 collective-permute-start.5
  26.7 2.6 slice_sine_fusion
  30.8 11.3 %project_in.1 = (bf16[512,512]{1,0:T(8,128)(2,1)}, bf16[2,512,512]{2,1,0:T(8,128)(2,1)}, bf16[512,1024]{1,0:T(8,128)(2,1)}, bf16[512,1024]{1,0:T(8,128)(2,1)}, f32[512,128]{1,0:T(8,128)}) custom-call(s32[2]{0:T(128)} %pad_add_fusion.1.index, bf16[512,512]{1,0:T(8,128)(2,1)} %refs_0_.1, bf16[512,512]{1,0:T(8,128)(2,1)} %copy-done.28, ...), custom_call_target="tpu_custom_call" | custom-call | flops 3221225472 | bytes 18874368 | tf_op jit(solution)/shard_map/project_in/pallas_call | solution.py:126
  42.1 2.9 collective-permute-start.7
  48.5 7.9 %project_halo.1.halo.refs_6_ = bf16[2,512,512]{2,1,0:T(8,128)(2,1)} custom-call(s32[2]{0:T(128)} %pad_add_fusion.1.index, bf16[512,512]{1,0:T(8,128)(2,1)} %copy-done.21, bf16[512,512]{1,0:T(8,128)(2,1)} %copy-done.29, bf16[512,512]{1,0:T(8,128)(2,1)} %copy-done.25, bf16[512,512]{1,0:T(8,128)(2,1)} %copy-done.30, f32[1,2048]{1,0:T(1,128)} %bitcast.125, ...), custom_call_target="tpu_custom_call" | custom-call | flops 2147483648 | bytes 10485760 | tf_op jit(solution)/shard_map/project_halo/pallas_call | solution.py:171
  56.4 15.8 %attend.1 = (bf16[512,512]{1,0:T(8,128)(2,1)}, f32[4,2,512]{2,1,0:T(2,128)}, bf16[512,1024]{1,0:T(8,128)(2,1)}, f32[512,1024]{1,0:T(8,128)}) custom-call(s32[4]{0:T(128)} %pad_add_fusion.order, bf16[512,512]{1,0:T(8,128)(2,1)} %get-tuple-element.69.query.refs_5_, bf16[2,512,512]{2,1,0:T(8,128)(2,1)} %project_halo.1.halo.refs_6_, ...), custom_call_target="tpu_custom_call" | custom-call | flops 2415919104 | bytes 8388608 | tf_op jit(solution)/shard_map/attend/pallas_call | solution.py:254
  72.4 2.7 collective-permute-done.8
  75.2 2.0 convert_add_fusion.3
  77.3 1.6 collective-permute-start.9
  78.9 19.4 %collective-permute-done.9 = bf16[512,512]{1,0:T(8,128)(2,1)S(1)} collective-permute-done((bf16[512,512]{1,0:T(8,128)(2,1)S(1)}, bf16[512,512]{1,0:T(8,128)(2,1)S(1)}, u32[]{:S(2)}, u32[]{:S(2)}) %collective-permute-start.9) | collective-permute-done | bytes 524320 | tf_op jit(solution)/shard_map/ppermute | solution.py:53
  100.9 2.5 collective-permute-done.11
  104.8 13.2 %collective-permute-done.13.refs_2_ = bf16[512,512]{1,0:T(8,128)(2,1)S(1)} collective-permute-done((bf16[512,512]{1,0:T(8,128)(2,1)}, bf16[512,512]{1,0:T(8,128)(2,1)S(1)}, u32[]{:S(2)}, u32[]{:S(2)}) %collective-permute-start.13) | collective-permute-done | bytes 524320 | tf_op jit(solution)/shard_map/ppermute | solution.py:53
  120.6 43.9 %own_units.1 = (bf16[512,2048]{1,0:T(8,128)(2,1)}, bf16[512,2048]{1,0:T(8,128)(2,1)}, bf16[512,2048]{1,0:T(8,128)(2,1)}, bf16[512,512]{1,0:T(8,128)(2,1)}, bf16[...) custom-call(s32[5]{0:T(128)} %stack.62.index, ...), custom_call_target="tpu_custom_call" | custom-call | flops 25769803776 | bytes 33554432 | tf_op jit(solution)/shard_map/own_units/pallas_call | solution.py:666
  165.1 2.4 collective-permute-done.17
  167.5 2.2 convert_add_fusion.1
  173.5 1.8 collective-permute-start.16
  175.3 9.8 %back_units.2 = (bf16[512,2048]{1,0:T(8,128)(2,1)}, bf16[512,512]{1,0:T(8,128)(2,1)}) custom-call(s32[5]{0:T(128)} %stack.62.index, bf16[4,2,2,512,512]{4,3,2,1,0:T(8,128)(2,1)} %bitcast.106, bf16[2048,2048]{1,0:T(8,128)(2,1)} %refs_2_.3), custom_call_target="tpu_custom_call" | custom-call | flops 4294967296 | bytes 12582912 | tf_op jit(solution)/shard_map/back_units/pallas_call | solution.py:547
  185.6 1.7 multiply_reduce_fusion
  188.7 7.6 %collective-permute-done.20 = f32[512]{0:T(512)S(1)} collective-permute-done((f32[512]{0:T(512)S(1)}, f32[512]{0:T(512)S(1)}, u32[]{:S(2)}, u32[]{:S(2)}) %collective-permute-start.20) | collective-permute-done | bytes 2080 | tf_op jit(solution)/shard_map/ppermute | solution.py:53
  196.4 3.1 fusion.49
  201.9 11.1 %collective-permute-done.22.refs_2_ = bf16[512,512]{1,0:T(8,128)(2,1)S(1)} collective-permute-done((bf16[512,512]{1,0:T(8,128)(2,1)}, bf16[512,512]{1,0:T(8,128)(2,1)S(1)}, u32[]{:S(2)}, u32[]{:S(2)}) %collective-permute-start.22) | collective-permute-done | bytes 524320 | tf_op jit(solution)/shard_map/ppermute | solution.py:53
  213.1 16.7 %far_units.2 = (bf16[512,2048]{1,0:T(8,128)(2,1)}, bf16[512,2048]{1,0:T(8,128)(2,1)}, bf16[512,2048]{1,0:T(8,128)(2,1)}, bf16[512,512]{1,0:T(8,128)(2,1)}) custom-call(s32[5]{0:T(128)} %stack.62.index, bf16[4,2,2,512,512]{4,3,2,1,0:T(8,128)(2,1)} %bitcast.126, bf16[512,2048]{1,0:T(8,128)(2,1)} %get-tuple-element.81.refs_1_, bf16[2048,2048]{1,0:T(8,128)(2,1)} %refs_3_.5, ...), custom_call_target="tpu_custom_call" | custom-call | flops 8589934592 | bytes 25165824 | tf_op jit(solution)/shard_map/far_units/pallas_call | solution.py:598
  230.8 20.9 %attend_back.1 = (bf16[512,512]{1,0:T(8,128)(2,1)}, bf16[2,512,512]{2,1,0:T(8,128)(2,1)}, f32[2,512,512]{2,1,0:T(8,128)}, bf16[512,1024]{1,0:T(8,128)(2,1)}, bf16[512,1024]{1,0:T(8,128)(2,1)}) custom-call(s32[2]{0:T(128)} %pad_add_fusion.1.index, bf16[512,512]{1,0:T(8,128)(2,1)} %get-tuple-element.86.refs_0_, bf16[512,512]{1,0:T(8,128)(2,1)} %copy-done.32, ...), custom_call_target="tpu_custom_call" | custom-call | flops 4429185024 | bytes 8388608 | tf_op jit(solution)/shard_map/attend_back/pallas_call | solution.py:340
  254.0 22.6 %back_units.3 = (bf16[1024,2048]{1,0:T(8,128)(2,1)}, bf16[1024,512]{1,0:T(8,128)(2,1)}) custom-call(s32[5]{0:T(128)} %stack.62.index, bf16[4,2,2,512,512]{4,3,2,1,0:T(8,128)(2,1)} %bitcast.107, bf16[4,2,2,512,512]{4,3,2,1,0:T(8,128)(2,1)} %bitcast.108, bf16[2048,2048]{1,0:T(8,128)(2,1)} %refs_2_.3), custom_call_target="tpu_custom_call" | custom-call | flops 8589934592 | bytes 16777216 | tf_op jit(solution)/shard_map/back_units/pallas_call | solution.py:547
  276.7 1.7 convolution_convert_fusion
  279.5 26.9 %far_units.3 = (bf16[1024,2048]{1,0:T(8,128)(2,1)}, bf16[1024,2048]{1,0:T(8,128)(2,1)}, bf16[1024,2048]{1,0:T(8,128)(2,1)}, bf16[1024,512]{1,0:T(8,128)(2,1)}) custom-call(s32[5]{0:T(128)} %stack.62.index, bf16[4,2,2,512,512]{4,3,2,1,0:T(8,128)(2,1)} %bitcast.127, bf16[4,2,2,512,512]{4,3,2,1,0:T(8,128)(2,1)} %bitcast.128, ...), custom_call_target="tpu_custom_call" | custom-call | flops 17179869184 | bytes 33554432 | tf_op jit(solution)/shard_map/far_units/pallas_call | solution.py:598
  307.5 4.6 finish_keys.1.refs_1_.refs_2_
  312.9 21.6 %ffn_grads.1 = (bf16[3,256,2048]{2,1,0:T(8,128)(2,1)}, f32[3,256,2048]{2,1,0:T(8,128)}) custom-call(s32[1]{0:T(128)} %bitcast.15.seat, bf16[512,512]{1,0:T(8,128)(2,1)} %get-tuple-element.101.refs_0_, bf16[512,512]{1,0:T(8,128)(2,1)} %get-tuple-element.102.refs_1_, bf16[1024,512]{1,0:T(8,128)(2,1)} %get-tuple-element.103.refs_2_, ...), custom_call_target="tpu_custom_call" | custom-call | flops 12884901888 | bytes 34603008 | tf_op jit(solution)/shard_map/ffn_grads/pallas_call | solution.py:737
  334.6 6.3 %partial_product.2 = bf16[512,1024]{1,0:T(8,128)(2,1)} custom-call(s32[2]{0:T(128)} %pad_add_fusion.3.order, bf16[512,512]{1,0:T(8,128)(2,1)} %get-tuple-element.91.refs_0_, bf16[2,512,512]{2,1,0:T(8,128)(2,1)} %finish_keys.1.refs_1_.refs_2_, bf16[2,512,512]{2,1,0:T(8,128)(2,1)} %finish_keys.1.refs_1_.refs_2_, bf16[2048,512]{1,0:T(8,128)(2,1)} %refs_3_.7, ...), custom_call_target="tpu_custom_call" | custom-call | flops 1610612736 | bytes 6291456 | tf_op jit(solution)/shard_map/partial_product/pallas_call | solution.py:464
  341.0 2.0 convert_add_fusion
  343.0 2.4 reshape.221
  346.9 5.1 %collective-permute-start.46 = (bf16[512,1,256]{2,0,1:T(8,128)(2,1)S(1)}, bf16[512,1,256]{2,0,1:T(8,128)(2,1)S(1)}, u32[]{:S(2)}, u32[]{:S(2)}) collective-permute-start(bf16[512,1,256]{2,0,1:T(8,128)(2,1)S(1)} %bitcast.113), channel_id=1, source_target_pairs={{0,24},{4,28},{8,0},{12,4},{16,8},{20,12},{24,16},{28,20},{1,25},{... | collective-permute-start | bytes 786440 | tf_op jit(solution)/shard_map/ppermute | solution.py:844
  354.4 2.8 constant_dynamic-slice_fusion.3
  360.3 14.9 %collective-permute-done.45 = bf16[512,1,256]{2,0,1:T(8,128)(2,1)S(1)} collective-permute-done((bf16[512,1,256]{2,0,1:T(8,128)(2,1)S(1)}, bf16[512,1,256]{2,0,1:T(8,128)(2,1)S(1)}, u32[]{:S(2)}, u32[]{:S(2)}) %collective-permute-start.45) | collective-permute-done | bytes 262176 | tf_op jit(solution)/shard_map/ppermute | solution.py:844
  375.2 2.6 collective-permute-start.38
  378.7 6.7 %partial_product.3 = (bf16[512,512]{1,0:T(8,128)(2,1)}, f32[512,512]{1,0:T(8,128)}) custom-call(s32[2]{0:T(128)} %pad_add_fusion.2.order, bf16[512,512]{1,0:T(8,128)(2,1)} %get-tuple-element.91.refs_0_, bf16[2,512,512]{2,1,0:T(8,128)(2,1)} %finish_keys.1.refs_1_.refs_2_, bf16[2,512,512]{2,1,0:T(8,128)(2,1)} %finish_keys.1.refs_1_.refs_2_, ...), custom_call_target="tpu_custom_call" | custom-call | flops 1610612736 | bytes 6291456 | tf_op jit(solution)/shard_map/partial_product/pallas_call | solution.py:464
  385.8 1.8 fusion.24
  388.4 1.8 fusion.23
  391.2 3.9 collective-permute-start.43
  395.1 3.7 collective-permute-done.38
  398.8 23.1 %collective-permute-start.41 = (bf16[1,256,1024]{2,1,0:T(8,128)(2,1)S(1)}, bf16[1,256,1024]{2,1,0:T(8,128)(2,1)S(1)}, u32[]{:S(2)}, u32[]{:S(2)}) collective-permute-start(bf16[1,256,1024]{2,1,0:T(8,128)(2,1)S(1)} %get-tuple-element.137), channel_id=1, source_target_pairs={{0,8},{4,12},{8,16},{12,20},{16,24},{20,28},{24,0},{28,4},{1,9},{5... | collective-permute-start | bytes 1572872 | tf_op jit(solution)/shard_map/ppermute | solution.py:844
  421.9 2.0 fusion.32
  424.5 1.6 collective-permute-start.31
  426.1 16.7 %collective-permute-done.42 = bf16[1,256,1024]{2,1,0:T(8,128)(2,1)S(1)} collective-permute-done((bf16[1,256,1024]{2,1,0:T(8,128)(2,1)S(1)}, bf16[1,256,1024]{2,1,0:T(8,128)(2,1)S(1)}, u32[]{:S(2)}, u32[]{:S(2)}) %collective-permute-start.42) | collective-permute-done | bytes 524320 | tf_op jit(solution)/shard_map/ppermute | solution.py:844
  446.8 3.5 collective-permute-start.33
  457.5 6.7 %add_grads.1 = (f32[256,2048]{1,0:T(8,128)}, f32[256,2048]{1,0:T(8,128)}, f32[2048,256]{1,0:T(8,128)}) custom-call(f32[3,256,2048]{2,1,0:T(8,128)} %get-tuple-element.123.keep, bf16[3,256,2048]{2,1,0:T(8,128)(2,1)} %collective-permute-done.47.got), custom_call_target="tpu_custom_call" | custom-call | flops 1572864 | bytes 15728640 | tf_op jit(solution)/shard_map/add_grads/pallas_call | solution.py:763
  (202 shorter events, 51.9 us)
Async XLA Ops:
  7.2 112.7 %all-gather.5.cloned.1.call-start = ((), (), s32[]{:S(2)}) async-start(), calls=%async_computation | async-start | bytes 8912896 | tf_op jit(solution)/shard_map/all_gather | solution.py:852
  7.2 15.2 %collective-permute-start.1 = (bf16[512,512]{1,0:T(8,128)(2,1)}, bf16[512,512]{1,0:T(8,128)(2,1)S(1)}, u32[]{:S(2)}, u32[]{:S(2)}) collective-permute-start(bf16[512,512]{1,0:T(8,128)(2,1)} %refs_0_.1), channel_id=1, source_target_pairs={{0,2},{1,3},{2,0},{3,1},{4,6},{5,7},{6,4},{7,5},{8,10},{9,11},{10,... | collective-permute-start | bytes 1572872 | tf_op jit(solution)/shard_map/ppermute | solution.py:53
  10.3 12.1 %collective-permute-start.3 = (bf16[512,512]{1,0:T(8,128)(2,1)}, bf16[512,512]{1,0:T(8,128)(2,1)S(1)}, u32[]{:S(2)}, u32[]{:S(2)}) collective-permute-start(bf16[512,512]{1,0:T(8,128)(2,1)} %refs_0_.1), channel_id=1, source_target_pairs={{4,8},{8,12},{20,24},{24,28},{5,9},{9,13},{21,25},{25,29},{6,10},{... | collective-permute-start | bytes 1572872 | tf_op jit(solution)/shard_map/ppermute | solution.py:850
  22.4 190.7 %all-gather.7.cloned.1.call-start = ((), (), s32[]{:S(2)}) async-start(), calls=%async_computation.1 | async-start | bytes 8912896 | tf_op jit(solution)/shard_map/all_gather | solution.py:872
  22.5 7.4 %collective-permute-start = (bf16[512,512]{1,0:T(8,128)(2,1)}, bf16[512,512]{1,0:T(8,128)(2,1)S(1)}, u32[]{:S(2)}, u32[]{:S(2)}) collective-permute-start(bf16[512,512]{1,0:T(8,128)(2,1)} %refs_0_.1), channel_id=1, source_target_pairs={{0,1},{1,0},{2,3},{3,2},{4,5},{5,4},{6,7},{7,6},{8,9},{9,8},{10,11... | collective-permute-start | bytes 1572872 | tf_op jit(solution)/shard_map/ppermute | solution.py:53
  24.2 5.7 %collective-permute-start.2 = (bf16[512,512]{1,0:T(8,128)(2,1)S(1)}, bf16[512,512]{1,0:T(8,128)(2,1)S(1)}, u32[]{:S(2)}, u32[]{:S(2)}) collective-permute-start(bf16[512,512]{1,0:T(8,128)(2,1)S(1)} %collective-permute-done.1.refs_2_), channel_id=1, source_target_pairs={{0,1},{1,0},{2,3},{3,2},{4,5},{5,4},{6,7},{7,6},{8,9},{9,8},{10,11... | collective-permute-start | bytes 1572872 | tf_op jit(solution)/shard_map/ppermute | solution.py:53
  24.9 20.1 %collective-permute-start.5 = (bf16[512,512]{1,0:T(8,128)(2,1)S(1)}, bf16[512,512]{1,0:T(8,128)(2,1)S(1)}, u32[]{:S(2)}, u32[]{:S(2)}) collective-permute-start(bf16[512,512]{1,0:T(8,128)(2,1)S(1)} %collective-permute-done.3.refs_0_), channel_id=1, source_target_pairs={{0,2},{1,3},{2,0},{3,1},{4,6},{5,7},{6,4},{7,5},{8,10},{9,11},{10,... | collective-permute-start | bytes 1572872 | tf_op jit(solution)/shard_map/ppermute | solution.py:53
  42.1 30.1 %collective-permute-start.7 = (bf16[512,1024]{1,0:T(8,128)(2,1)}, bf16[512,1024]{1,0:T(8,128)(2,1)S(1)}, u32[]{:S(2)}, u32[]{:S(2)}) collective-permute-start(bf16[512,1024]{1,0:T(8,128)(2,1)} %get-tuple-element.73), channel_id=1, source_target_pairs={{0,4},{4,0},{1,5},{5,1},{2,6},{6,2},{3,7},{7,3},{8,12},{12,8},{9,1... | collective-permute-start | bytes 3145736 | tf_op jit(solution)/shard_map/ppermute | solution.py:53
  45.1 1.9 collective-permute-start.4
  45.1 2.6 collective-permute-start.6
  72.2 2.9 collective-permute-start.8
  77.3 21.0 %collective-permute-start.9 = (bf16[512,512]{1,0:T(8,128)(2,1)S(1)}, bf16[512,512]{1,0:T(8,128)(2,1)S(1)}, u32[]{:S(2)}, u32[]{:S(2)}) collective-permute-start(bf16[512,512]{1,0:T(8,128)(2,1)S(1)} %slice.133), channel_id=1, source_target_pairs={{0,2},{1,3},{2,0},{3,1},{4,6},{5,7},{6,4},{7,5},{8,10},{9,11},{10,... | collective-permute-start | bytes 1572872 | tf_op jit(solution)/shard_map/ppermute | solution.py:53
  98.6 1.2 collective-permute-start.10
  99.8 3.6 collective-permute-start.11
  104.4 13.5 %collective-permute-start.13 = (bf16[512,512]{1,0:T(8,128)(2,1)}, bf16[512,512]{1,0:T(8,128)(2,1)S(1)}, u32[]{:S(2)}, u32[]{:S(2)}) collective-permute-start(bf16[512,512]{1,0:T(8,128)(2,1)} %multiply_convert_fusion.refs_0_), channel_id=1, source_target_pairs={{0,2},{1,3},{2,0},{3,1},{4,6},{5,7},{6,4},{7,5},{8,10},{9,11},{10,... | collective-permute-start | bytes 1572872 | tf_op jit(solution)/shard_map/ppermute | solution.py:53
  104.8 13.9 %collective-permute-start.12 = (bf16[512,512]{1,0:T(8,128)(2,1)}, bf16[512,512]{1,0:T(8,128)(2,1)S(1)}, u32[]{:S(2)}, u32[]{:S(2)}) collective-permute-start(bf16[512,512]{1,0:T(8,128)(2,1)} %multiply_convert_fusion.refs_0_), channel_id=1, source_target_pairs={{0,1},{1,0},{2,3},{3,2},{4,5},{5,4},{6,7},{7,6},{8,9},{9,8},{10,11... | collective-permute-start | bytes 1572872 | tf_op jit(solution)/shard_map/ppermute | solution.py:53
  117.9 1.9 collective-permute-start.14
  164.6 2.9 collective-permute-start.17
  164.8 6.0 %collective-permute-start.15 = (bf16[512,1024]{1,0:T(8,128)(2,1)}, bf16[512,1024]{1,0:T(8,128)(2,1)S(1)}, u32[]{:S(2)}, u32[]{:S(2)}) collective-permute-start(bf16[512,1024]{1,0:T(8,128)(2,1)} %get-tuple-element.77), channel_id=1, source_target_pairs={{0,1},{1,0},{2,3},{3,2},{4,5},{5,4},{6,7},{7,6},{8,9},{9,8},{10,11... | collective-permute-start | bytes 3145736 | tf_op jit(solution)/shard_map/ppermute | solution.py:53
  170.6 15.1 %collective-permute-start.18 = (bf16[512,512]{1,0:T(8,128)(2,1)}, bf16[512,512]{1,0:T(8,128)(2,1)}, u32[]{:S(2)}, u32[]{:S(2)}) collective-permute-start(bf16[512,512]{1,0:T(8,128)(2,1)} %slice.131), channel_id=1, source_target_pairs={{0,2},{1,3},{2,0},{3,1},{4,6},{5,7},{6,4},{7,5},{8,10},{9,11},{10,... | collective-permute-start | bytes 1572872 | tf_op jit(solution)/shard_map/ppermute | solution.py:53
  173.5 22.9 %collective-permute-start.16 = (bf16[512,512]{1,0:T(8,128)(2,1)}, bf16[512,512]{1,0:T(8,128)(2,1)}, u32[]{:S(2)}, u32[]{:S(2)}) collective-permute-start(bf16[512,512]{1,0:T(8,128)(2,1)} %slice.132), channel_id=1, source_target_pairs={{0,2},{1,3},{2,0},{3,1},{4,6},{5,7},{6,4},{7,5},{8,10},{9,11},{10,... | collective-permute-start | bytes 1572872 | tf_op jit(solution)/shard_map/ppermute | solution.py:53
  188.5 7.8 %collective-permute-start.20 = (f32[512]{0:T(512)S(1)}, f32[512]{0:T(512)S(1)}, u32[]{:S(2)}, u32[]{:S(2)}) collective-permute-start(f32[512]{0:T(512)S(1)} %add.272), channel_id=1, source_target_pairs={{0,2},{1,3},{2,0},{3,1},{4,6},{5,7},{6,4},{7,5},{8,10},{9,11},{10,... | collective-permute-start | bytes 6152 | tf_op jit(solution)/shard_map/ppermute | solution.py:53
  199.5 13.6 %collective-permute-start.22 = (bf16[512,512]{1,0:T(8,128)(2,1)}, bf16[512,512]{1,0:T(8,128)(2,1)S(1)}, u32[]{:S(2)}, u32[]{:S(2)}) collective-permute-start(bf16[512,512]{1,0:T(8,128)(2,1)} %get-tuple-element.86.refs_0_), channel_id=1, source_target_pairs={{0,2},{1,3},{2,0},{3,1},{4,6},{5,7},{6,4},{7,5},{8,10},{9,11},{10,... | collective-permute-start | bytes 1572872 | tf_op jit(solution)/shard_map/ppermute | solution.py:53
  201.8 27.9 %collective-permute-start.21 = (bf16[512,512]{1,0:T(8,128)(2,1)}, bf16[512,512]{1,0:T(8,128)(2,1)S(1)}, u32[]{:S(2)}, u32[]{:S(2)}) collective-permute-start(bf16[512,512]{1,0:T(8,128)(2,1)} %get-tuple-element.86.refs_0_), channel_id=1, source_target_pairs={{0,1},{1,0},{2,3},{3,2},{4,5},{5,4},{6,7},{7,6},{8,9},{9,8},{10,11... | collective-permute-start | bytes 1572872 | tf_op jit(solution)/shard_map/ppermute | solution.py:53
  213.1 16.7 %collective-permute-start.23 = (bf16[512,512]{1,0:T(8,128)(2,1)S(1)}, bf16[512,512]{1,0:T(8,128)(2,1)S(1)}, u32[]{:S(2)}, u32[]{:S(2)}) collective-permute-start(bf16[512,512]{1,0:T(8,128)(2,1)S(1)} %collective-permute-done.22.refs_2_), channel_id=1, source_target_pairs={{0,1},{1,0},{2,3},{3,2},{4,5},{5,4},{6,7},{7,6},{8,9},{9,8},{10,11... | collective-permute-start | bytes 1572872 | tf_op jit(solution)/shard_map/ppermute | solution.py:53
  251.7 82.9 %collective-permute-start.26 = (bf16[512,512]{1,0:T(8,128)(2,1)}, bf16[512,512]{1,0:T(8,128)(2,1)S(1)}, u32[]{:S(2)}, u32[]{:S(2)}) collective-permute-start(bf16[512,512]{1,0:T(8,128)(2,1)} %get-tuple-element.91.refs_0_), channel_id=1, source_target_pairs={{0,4},{4,0},{1,5},{5,1},{2,6},{6,2},{3,7},{7,3},{8,12},{12,8},{9,1... | collective-permute-start | bytes 1572872 | tf_op jit(solution)/shard_map/ppermute | solution.py:53
  253.2 53.3 %collective-permute-start.24 = (bf16[2,512,512]{2,1,0:T(8,128)(2,1)}, bf16[2,512,512]{2,1,0:T(8,128)(2,1)S(1)}, u32[]{:S(2)}, u32[]{:S(2)}) collective-permute-start(bf16[2,512,512]{2,1,0:T(8,128)(2,1)} %get-tuple-element.93), channel_id=1, source_target_pairs={{8,4},{12,8},{24,20},{28,24},{9,5},{13,9},{25,21},{29,25},{10,6},{... | collective-permute-start | bytes 3145736 | tf_op jit(solution)/shard_map/ppermute | solution.py:908
  278.4 56.2 %collective-permute-start.25 = (bf16[512,1024]{1,0:T(8,128)(2,1)}, bf16[512,1024]{1,0:T(8,128)(2,1)S(1)}, u32[]{:S(2)}, u32[]{:S(2)}) collective-permute-start(bf16[512,1024]{1,0:T(8,128)(2,1)} %convolution_convert_fusion), channel_id=1, source_target_pairs={{0,4},{4,0},{1,5},{5,1},{2,6},{6,2},{3,7},{7,3},{8,12},{12,8},{9,1... | collective-permute-start | bytes 3145736 | tf_op jit(solution)/shard_map/ppermute | solution.py:53
  312.0 73.3 %collective-permute-start.40 = (bf16[2,512,512]{2,1,0:T(8,128)(2,1)}, bf16[2,512,512]{2,1,0:T(8,128)(2,1)}, u32[]{:S(2)}, u32[]{:S(2)}) collective-permute-start(bf16[2,512,512]{2,1,0:T(8,128)(2,1)} %finish_keys.1.refs_1_.refs_2_), channel_id=1, source_target_pairs={{0,4},{4,0},{1,5},{5,1},{2,6},{6,2},{3,7},{7,3},{8,12},{12,8},{9,1... | collective-permute-start | bytes 3145736 | tf_op jit(solution)/shard_map/ppermute | solution.py:53
  340.9 37.7 %collective-permute-start.27 = (bf16[512,1024]{1,0:T(8,128)(2,1)}, bf16[512,1024]{1,0:T(8,128)(2,1)}, u32[]{:S(2)}, u32[]{:S(2)}) collective-permute-start(bf16[512,1024]{1,0:T(8,128)(2,1)} %partial_product.2), channel_id=1, source_target_pairs={{0,1},{1,0},{2,3},{3,2},{4,5},{5,4},{6,7},{7,6},{8,9},{9,8},{10,11... | collective-permute-start | bytes 3145736 | tf_op jit(solution)/shard_map/ppermute | solution.py:53
  346.9 11.8 %collective-permute-start.46 = (bf16[512,1,256]{2,0,1:T(8,128)(2,1)S(1)}, bf16[512,1,256]{2,0,1:T(8,128)(2,1)S(1)}, u32[]{:S(2)}, u32[]{:S(2)}) collective-permute-start(bf16[512,1,256]{2,0,1:T(8,128)(2,1)S(1)} %bitcast.113), channel_id=1, source_target_pairs={{0,24},{4,28},{8,0},{12,4},{16,8},{20,12},{24,16},{28,20},{1,25},{... | collective-permute-start | bytes 786440 | tf_op jit(solution)/shard_map/ppermute | solution.py:844
  352.1 23.1 %collective-permute-start.45 = (bf16[512,1,256]{2,0,1:T(8,128)(2,1)S(1)}, bf16[512,1,256]{2,0,1:T(8,128)(2,1)S(1)}, u32[]{:S(2)}, u32[]{:S(2)}) collective-permute-start(bf16[512,1,256]{2,0,1:T(8,128)(2,1)S(1)} %bitcast.112), channel_id=1, source_target_pairs={{0,16},{4,20},{8,24},{12,28},{16,0},{20,4},{24,8},{28,12},{1,17},{... | collective-permute-start | bytes 786440 | tf_op jit(solution)/shard_map/ppermute | solution.py:844
  352.2 23.0 %collective-permute-start.44 = (bf16[512,1,256]{2,0,1:T(8,128)(2,1)S(1)}, bf16[512,1,256]{2,0,1:T(8,128)(2,1)S(1)}, u32[]{:S(2)}, u32[]{:S(2)}) collective-permute-start(bf16[512,1,256]{2,0,1:T(8,128)(2,1)S(1)} %bitcast.111), channel_id=1, source_target_pairs={{0,8},{4,12},{8,16},{12,20},{16,24},{20,28},{24,0},{28,4},{1,9},{5... | collective-permute-start | bytes 786440 | tf_op jit(solution)/shard_map/ppermute | solution.py:844
  358.7 98.7 %collective-permute-start.47 = (bf16[3,256,2048]{2,1,0:T(8,128)(2,1)}, bf16[3,256,2048]{2,1,0:T(8,128)(2,1)}, u32[]{:S(2)}, u32[]{:S(2)}) collective-permute-start(bf16[3,256,2048]{2,1,0:T(8,128)(2,1)} %get-tuple-element.115), channel_id=1, source_target_pairs={{0,4},{4,0},{8,12},{12,8},{16,20},{20,16},{24,28},{28,24},{1,5},{5... | collective-permute-start | bytes 9437192 | tf_op jit(solution)/shard_map/ppermute | solution.py:812
  375.2 16.0 %collective-permute-start.39 = (bf16[1,256,512]{2,1,0:T(8,128)(2,1)S(1)}, bf16[1,256,512]{2,1,0:T(8,128)(2,1)S(1)}, u32[]{:S(2)}, u32[]{:S(2)}) collective-permute-start(bf16[1,256,512]{2,1,0:T(8,128)(2,1)S(1)} %get-tuple-element.144), channel_id=1, source_target_pairs={{0,24},{4,28},{8,0},{12,4},{16,8},{20,12},{24,16},{28,20},{1,25},{... | collective-permute-start | bytes 786440 | tf_op jit(solution)/shard_map/ppermute | solution.py:844
  375.2 23.6 %collective-permute-start.38 = (bf16[1,256,512]{2,1,0:T(8,128)(2,1)S(1)}, bf16[1,256,512]{2,1,0:T(8,128)(2,1)S(1)}, u32[]{:S(2)}, u32[]{:S(2)}) collective-permute-start(bf16[1,256,512]{2,1,0:T(8,128)(2,1)S(1)} %get-tuple-element.145), channel_id=1, source_target_pairs={{0,16},{4,20},{8,24},{12,28},{16,0},{20,4},{24,8},{28,12},{1,17},{... | collective-permute-start | bytes 786440 | tf_op jit(solution)/shard_map/ppermute | solution.py:844
  378.7 20.1 %collective-permute-start.37 = (bf16[1,256,512]{2,1,0:T(8,128)(2,1)S(1)}, bf16[1,256,512]{2,1,0:T(8,128)(2,1)}, u32[]{:S(2)}, u32[]{:S(2)}) collective-permute-start(bf16[1,256,512]{2,1,0:T(8,128)(2,1)S(1)} %get-tuple-element.143), channel_id=1, source_target_pairs={{0,8},{4,12},{8,16},{12,20},{16,24},{20,28},{24,0},{28,4},{1,9},{5... | collective-permute-start | bytes 786440 | tf_op jit(solution)/shard_map/ppermute | solution.py:844
  385.4 38.6 %collective-permute-start.28 = (bf16[512,512]{1,0:T(8,128)(2,1)}, bf16[512,512]{1,0:T(8,128)(2,1)S(1)}, u32[]{:S(2)}, u32[]{:S(2)}) collective-permute-start(bf16[512,512]{1,0:T(8,128)(2,1)} %get-tuple-element.118), channel_id=1, source_target_pairs={{0,2},{1,3},{2,0},{3,1},{4,6},{5,7},{6,4},{7,5},{8,10},{9,11},{10,... | collective-permute-start | bytes 1572872 | tf_op jit(solution)/shard_map/ppermute | solution.py:53
  391.2 33.3 %collective-permute-start.43 = (bf16[1,256,1024]{2,1,0:T(8,128)(2,1)S(1)}, bf16[1,256,1024]{2,1,0:T(8,128)(2,1)S(1)}, u32[]{:S(2)}, u32[]{:S(2)}) collective-permute-start(bf16[1,256,1024]{2,1,0:T(8,128)(2,1)S(1)} %get-tuple-element.139), channel_id=1, source_target_pairs={{0,24},{4,28},{8,0},{12,4},{16,8},{20,12},{24,16},{28,20},{1,25},{... | collective-permute-start | bytes 1572872 | tf_op jit(solution)/shard_map/ppermute | solution.py:844
  398.8 44.0 %collective-permute-start.42 = (bf16[1,256,1024]{2,1,0:T(8,128)(2,1)S(1)}, bf16[1,256,1024]{2,1,0:T(8,128)(2,1)S(1)}, u32[]{:S(2)}, u32[]{:S(2)}) collective-permute-start(bf16[1,256,1024]{2,1,0:T(8,128)(2,1)S(1)} %get-tuple-element.138), channel_id=1, source_target_pairs={{0,16},{4,20},{8,24},{12,28},{16,0},{20,4},{24,8},{28,12},{1,17},{... | collective-permute-start | bytes 1572872 | tf_op jit(solution)/shard_map/ppermute | solution.py:844
  398.8 44.0 %collective-permute-start.41 = (bf16[1,256,1024]{2,1,0:T(8,128)(2,1)S(1)}, bf16[1,256,1024]{2,1,0:T(8,128)(2,1)S(1)}, u32[]{:S(2)}, u32[]{:S(2)}) collective-permute-start(bf16[1,256,1024]{2,1,0:T(8,128)(2,1)S(1)} %get-tuple-element.137), channel_id=1, source_target_pairs={{0,8},{4,12},{8,16},{12,20},{16,24},{20,28},{24,0},{28,4},{1,9},{5... | collective-permute-start | bytes 1572872 | tf_op jit(solution)/shard_map/ppermute | solution.py:844
  424.4 21.4 %collective-permute-start.29 = (f32[512]{0:T(512)S(1)}, f32[512]{0:T(512)S(1)}, u32[]{:S(2)}, u32[]{:S(2)}) collective-permute-start(f32[512]{0:T(512)S(1)} %get-tuple-element.130), channel_id=1, source_target_pairs={{0,1},{1,0},{2,3},{3,2},{4,5},{5,4},{6,7},{7,6},{8,9},{9,8},{10,11... | collective-permute-start | bytes 6152 | tf_op jit(solution)/shard_map/ppermute | solution.py:53
  424.5 18.6 %collective-permute-start.31 = (f32[2,512]{1,0:T(2,128)S(1)}, f32[2,512]{1,0:T(2,128)S(1)}, u32[]{:S(2)}, u32[]{:S(2)}) collective-permute-start(f32[2,512]{1,0:T(2,128)S(1)} %pad_maximum_fusion), channel_id=1, source_target_pairs={{0,4},{4,0},{8,12},{12,8},{16,20},{20,16},{24,28},{28,24},{1,5},{5... | collective-permute-start | bytes 12296 | tf_op jit(solution)/shard_map/ppermute | solution.py:53
  443.2 3.7 collective-permute-start.32
  445.8 4.6 collective-permute-start.30
  446.8 5.1 %collective-permute-start.33 = (f32[2,512]{1,0:T(2,128)S(1)}, f32[2,512]{1,0:T(2,128)S(1)}, u32[]{:S(2)}, u32[]{:S(2)}) collective-permute-start(f32[2,512]{1,0:T(2,128)S(1)} %fusion.65), channel_id=1, source_target_pairs={{0,16},{4,20},{8,24},{12,28},{16,0},{20,4},{24,8},{28,12},{1,17},{... | collective-permute-start | bytes 12296 | tf_op jit(solution)/shard_map/ppermute | solution.py:53
  451.9 3.8 collective-permute-start.34
  452.0 3.7 collective-permute-start.35
  (37 other events, 308.4 us)
Sparse Core Ops, SparseCore 0:
  22.5 85.9 all-gather.4
  111.3 73.0 all-gather.6
